TPU v7x, 128 devices: a whole 4x4x4 slice. The times are simulated.
128 devices in a mesh: pipe: 4 (over z_hi, core), dp: 32 (over z_lo, x, y).
Axes of the slice: x: 4, y: 4, z: 4 (z_hi: 2, z_lo: 2; z = z_hi * 2 + z_lo), core: 2. Of those that a mesh axis runs over, the one named last changes fastest.
Arguments:
- frames_in: bfloat16 [64, 750, 1536], P('dp'), may hold values from -6 to 6
- lengths: int32 [64], P('dp'), may hold values from 375 to 750, as said below
- norm_gain: float32 [2, 4, 1536], P(None, 'pipe'), may hold values from 0.25 to 1.75
- lift_weight: bfloat16 [2, 4, 1536, 3072], P(None, 'pipe', 'dp'), may hold values from -0.15625 to 0.15625
- depth_kernel: float32 [2, 4, 31, 1536], P(None, 'pipe'), may hold values from -1 to 1
- out_gain: float32 [2, 4, 1536], P(None, 'pipe'), may hold values from 0.25 to 1.75
Outputs:
- frames_out: bfloat16 [64, 750, 1536], P('dp', None, 'pipe')
Inputs may be any that keep to these rules, and one draw needn't show every extreme that they name: `lengths`: valid frames of each clip; in every draw at least one clip has all its frames valid.
All inputs are finite; a program needn't handle non-finite values.
Results may differ from a plain program's by a relative error of at most 0.022.
Values may be sent and summed in bfloat16 or wider, within the bound.
A program may use at most 128 MiB of HBM per device.

v0:
```python
import jax
import jax.numpy as jnp
from jax import lax
from jax.sharding import PartitionSpec as P


def passed_along(block, axis, distance):
    devices = range(lax.axis_size(axis))
    route = [((i - distance) % len(devices), i) for i in devices]
    return lax.ppermute(block, axis, route)


def layer_norm(values):
    centred = values - jnp.mean(values, axis=-1, keepdims=True)
    return centred * lax.rsqrt(jnp.mean(centred * centred, axis=-1, keepdims=True) + 1e-05)


def conv_module(current, valid_mask, gain_in, lift_weight, kernel, gain_out):
    model_width = current.shape[-1]
    frame_count = current.shape[0]
    kernel_taps = kernel.shape[0]
    half_width = (kernel_taps - 1) // 2
    values = current.astype(jnp.float32)
    normed = (layer_norm(values) * gain_in).astype(jnp.bfloat16)
    lifted = jnp.dot(normed, lift_weight, preferred_element_type=jnp.float32)
    gated_rows = (
        lifted[:, :model_width] * jax.nn.sigmoid(lifted[:, model_width:]) * valid_mask[:, None]
    )
    padded = jnp.pad(gated_rows, ((half_width, half_width), (0, 0)))
    mixed_rows = padded[0:frame_count] * kernel[0]
    for offset in range(1, kernel_taps):
        mixed_rows = mixed_rows + padded[offset : offset + frame_count] * kernel[offset]
    branch = jax.nn.silu(layer_norm(mixed_rows) * gain_out)
    return (values + valid_mask[:, None] * branch).astype(jnp.bfloat16)


def on_device(frames_in, lengths, norm_gain, lift_weight, depth_kernel, out_gain):
    sections = lax.axis_size("pipe")
    section = lax.axis_index("pipe")
    micro_count = frames_in.shape[0]
    frame_count = frames_in.shape[1]
    model_width = frames_in.shape[2]
    virtual = lift_weight.shape[0]
    group_size = min(micro_count, sections)
    per_round = group_size + virtual * sections - 1
    total_ticks = micro_count // group_size * per_round
    positions = jnp.arange(frame_count, dtype=jnp.int32)

    def run_tick(tick, current, outputs, weights):
        round_index = tick // per_round
        local_tick = tick % per_round
        offset = local_tick - section
        virt_index = jnp.floor_divide(offset, sections)
        slot_index = jnp.mod(offset, sections)
        active = (offset >= 0) & (virt_index < virtual) & (slot_index < group_size)
        clip_index = jnp.clip(round_index * group_size + slot_index, 0, micro_count - 1)
        virt_safe = jnp.clip(virt_index, 0, virtual - 1)
        fresh = lax.dynamic_index_in_dim(frames_in, clip_index, 0, keepdims=False)
        incoming = jnp.where((section == 0) & (virt_safe == 0), fresh, current)
        length_here = lax.dynamic_index_in_dim(lengths, clip_index, 0, keepdims=False)
        valid_mask = (positions < length_here).astype(jnp.float32)

        def compute_first():
            return conv_module(
                incoming,
                valid_mask,
                norm_gain[0, 0],
                weights[0],
                depth_kernel[0, 0],
                out_gain[0, 0],
            )

        def compute_second():
            return conv_module(
                incoming,
                valid_mask,
                norm_gain[1, 0],
                weights[1],
                depth_kernel[1, 0],
                out_gain[1, 0],
            )

        def compute_module():
            return lax.cond(virt_safe == 0, compute_first, compute_second)

        def pass_along():
            return incoming

        result = lax.cond(active, compute_module, pass_along)
        store = active & (section == sections - 1) & (virt_safe == virtual - 1)
        previous = lax.dynamic_index_in_dim(outputs, clip_index, 0, keepdims=False)
        outputs = lax.dynamic_update_index_in_dim(
            outputs, jnp.where(store, result, previous), clip_index, 0
        )
        return (result, outputs)

    carry = (
        jnp.zeros((frame_count, model_width), jnp.bfloat16),
        jnp.zeros((micro_count, frame_count, model_width), jnp.bfloat16),
    )
    gathered = lax.all_gather(lift_weight, "dp", axis=2, tiled=True)[:, 0]
    weights = (gathered[0], gathered[1])

    def one_step(tick, state_pair):
        result, outputs = run_tick(tick, state_pair[0], state_pair[1], weights)
        return (passed_along(result, "pipe", 1), outputs)

    carry = lax.fori_loop(0, total_ticks - 1, one_step, carry)
    result, outputs = run_tick(total_ticks - 1, carry[0], carry[1], weights)
    quarter = model_width // sections
    pieces = outputs.reshape(micro_count, frame_count, sections, quarter)
    received = lax.all_to_all(pieces, "pipe", split_axis=2, concat_axis=2, tiled=True)
    return received[:, :, sections - 1, :]


def solution(mesh):
    return jax.shard_map(
        on_device,
        mesh=mesh,
        in_specs=(
            P("dp", None, None),
            P("dp"),
            P(None, "pipe", None),
            P(None, "pipe", "dp", None),
            P(None, "pipe", None, None),
            P(None, "pipe", None),
        ),
        out_specs=P("dp", None, "pipe"),
        check_vma=False,
    )
```

profile of v0, /device:TPU:1, one launch (start us, length us, event | category | flops | bytes accessed | tf_op | source)
XLA Modules:
  0.0 1284.1 jit_solution(3878424435524869062)
XLA Ops:
  15.3 209.1 %all-gather.2.cloned.1.call-done = bf16[2,1,1536,3072]{3,2,1,0:T(8,128)(2,1)} async-done(((bf16[2,1,48,3072]{3,2,1,0:T(8,128)(2,1)}), bf16[2,1,1536,3072]{3,2,1,0:T(8,128)(2,1)}) %all-gather.2.cloned.1.call-update) | async-done | bytes 18874384 | tf_op jit(solution)/shard_map/all_gather | solution.py:101
  242.8 880.7 %while.19 = (s32[]{:T(128)}, bf16[750,1536]{1,0:T(8,128)(2,1)}, bf16[2,750,1536]{2,1,0:T(8,128)(2,1)}, s32[]{:T(128)}, pred[]{:T(512)}, /*index=5*/bf16[2,750,15...) while((s32[]{:T(128)}, bf16[750,1536]{1,0:T(8,128)(2,1)}, ...), condition=%wide.region_13.14_spmd.clone, body=%wide.region_0.13_spmd.clone.sunk | while | flops 7186179072 | bytes 109187496 | solution.py:108
  253.9 83.3 %collective-permute-done = bf16[750,1536]{1,0:T(8,128)(2,1)} collective-permute-done((bf16[750,1536]{1,0:T(8,128)(2,1)S(1)}, bf16[750,1536]{1,0:T(8,128)(2,1)}, u32[]{:S(2)}, u32[]{:S(2)}) %collective-permute-start) | collective-permute-done | bytes 2304032 | tf_op jit(solution)/shard_map/while/body/eval_jaxpr/ppermute | solution.py:10
  341.1 86.2 %conditional.15 = (bf16[750,1536]{1,0:T(8,128)(2,1)S(1)}) conditional(s32[]{:T(128)} %convert_element_type.146, bf16[750,1536]{1,0:T(8,128)(2,1)S(1)} %bitcast_select_fusion.5, (s32[]{:T(128)}, bf16[750,1536]{1,0:T(8,128)(2,1)S(1)}, f32[750]{0:T(1024)S(1)}, f32[2,1,1536]{2,1,0:T(1,128)S(1)}, bf16[1536,3072]{1,0:T(8,128)(2,1)}, ...), branch_computations={%region_1.1_spmd, %region_2.12_spmd} | conditional | flops 7183873536 | bytes 81529584 | solution.py:89
  341.1 86.2 %conditional.2 = (bf16[750,1536]{1,0:T(8,128)(2,1)S(1)}) conditional(s32[]{:T(128)} %convert_element_type.61, (bf16[750,1536]{1,0:T(8,128)(2,1)S(1)}, f32[750]{0:T(1024)S(1)}, f32[2,1,1536]{2,1,0:T(1,128)S(1)}, bf16[1536,3072]{1,0:T(8,128)(2,1)}, f32[2,1,31,1536]{3,2,1,0:T(8,128)S(1)}, /*index=5*/f32[2,1,1536]{2,1,0:T(1,128)S(1)}) %tuple.60, ...), branch_computations={%region_3.6_spmd, %region_8.11_spmd} | conditional | flops 7183873536 | bytes 81529472
  355.9 64.6 %fusion.165 = (f32[750]{0:T(1024)S(1)}, f32[750,1536]{1,0:T(8,128)}) fusion(f32[1536]{0:T(1024)S(1)} %get-tuple-element.626, f32[1536]{0:T(1024)S(1)} %get-tuple-element.627, f32[1536]{0:T(1024)S(1)} %get-tuple-element.628, f32[1536]{0:T(1024)S(1)} %get-tuple-element.629, f32[1536]{0:T(1024)S(1)} %get-tuple-element.630, f32[1536]{0:T(1024)S(1)} %get-tuple-element.631, ...), kind=kLoop, calls=%fused_computation.397 | loop fusion | flops 71423248 | bytes 9409464 | tf_op jit(solution)/shard_map/while/body/eval_jaxpr/cond/branch_1_fun/cond/branch_1_fun/reduce_sum | solution.py:14
  431.2 24.8 %collective-permute-done = bf16[750,1536]{1,0:T(8,128)(2,1)} collective-permute-done((bf16[750,1536]{1,0:T(8,128)(2,1)S(1)}, bf16[750,1536]{1,0:T(8,128)(2,1)}, u32[]{:S(2)}, u32[]{:S(2)}) %collective-permute-start) | collective-permute-done | bytes 2304032 | tf_op jit(solution)/shard_map/while/body/eval_jaxpr/ppermute | solution.py:10
  459.9 86.2 %conditional.15 = (bf16[750,1536]{1,0:T(8,128)(2,1)S(1)}) conditional(s32[]{:T(128)} %convert_element_type.146, bf16[750,1536]{1,0:T(8,128)(2,1)S(1)} %bitcast_select_fusion.5, (s32[]{:T(128)}, bf16[750,1536]{1,0:T(8,128)(2,1)S(1)}, f32[750]{0:T(1024)S(1)}, f32[2,1,1536]{2,1,0:T(1,128)S(1)}, bf16[1536,3072]{1,0:T(8,128)(2,1)}, ...), branch_computations={%region_1.1_spmd, %region_2.12_spmd} | conditional | flops 7183873536 | bytes 81529584 | solution.py:89
  459.9 86.2 %conditional.2 = (bf16[750,1536]{1,0:T(8,128)(2,1)S(1)}) conditional(s32[]{:T(128)} %convert_element_type.61, (bf16[750,1536]{1,0:T(8,128)(2,1)S(1)}, f32[750]{0:T(1024)S(1)}, f32[2,1,1536]{2,1,0:T(1,128)S(1)}, bf16[1536,3072]{1,0:T(8,128)(2,1)}, f32[2,1,31,1536]{3,2,1,0:T(8,128)S(1)}, /*index=5*/f32[2,1,1536]{2,1,0:T(1,128)S(1)}) %tuple.60, ...), branch_computations={%region_3.6_spmd, %region_8.11_spmd} | conditional | flops 7183873536 | bytes 81529472
  474.8 64.6 %fusion.165 = (f32[750]{0:T(1024)S(1)}, f32[750,1536]{1,0:T(8,128)}) fusion(f32[1536]{0:T(1024)S(1)} %get-tuple-element.626, f32[1536]{0:T(1024)S(1)} %get-tuple-element.627, f32[1536]{0:T(1024)S(1)} %get-tuple-element.628, f32[1536]{0:T(1024)S(1)} %get-tuple-element.629, f32[1536]{0:T(1024)S(1)} %get-tuple-element.630, f32[1536]{0:T(1024)S(1)} %get-tuple-element.631, ...), kind=kLoop, calls=%fused_computation.397 | loop fusion | flops 71423248 | bytes 9409464 | tf_op jit(solution)/shard_map/while/body/eval_jaxpr/cond/branch_1_fun/cond/branch_1_fun/reduce_sum | solution.py:14
  550.7 21.4 %collective-permute-done = bf16[750,1536]{1,0:T(8,128)(2,1)} collective-permute-done((bf16[750,1536]{1,0:T(8,128)(2,1)S(1)}, bf16[750,1536]{1,0:T(8,128)(2,1)}, u32[]{:S(2)}, u32[]{:S(2)}) %collective-permute-start) | collective-permute-done | bytes 2304032 | tf_op jit(solution)/shard_map/while/body/eval_jaxpr/ppermute | solution.py:10
  576.0 90.3 %collective-permute-start = (bf16[750,1536]{1,0:T(8,128)(2,1)S(1)}, bf16[750,1536]{1,0:T(8,128)(2,1)}, u32[]{:S(2)}, u32[]{:S(2)}) collective-permute-start(bf16[750,1536]{1,0:T(8,128)(2,1)S(1)} %get-tuple-element.904), channel_id=1, source_target_pairs={{96,0},{0,32},{32,64},{64,96},{97,1},{1,33},{33,65},{65,97},{98,2}... | collective-permute-start | bytes 6912008 | tf_op jit(solution)/shard_map/while/body/eval_jaxpr/ppermute | solution.py:10
  670.2 21.4 %collective-permute-done = bf16[750,1536]{1,0:T(8,128)(2,1)} collective-permute-done((bf16[750,1536]{1,0:T(8,128)(2,1)S(1)}, bf16[750,1536]{1,0:T(8,128)(2,1)}, u32[]{:S(2)}, u32[]{:S(2)}) %collective-permute-start) | collective-permute-done | bytes 2304032 | tf_op jit(solution)/shard_map/while/body/eval_jaxpr/ppermute | solution.py:10
  703.6 58.2 %collective-permute-done = bf16[750,1536]{1,0:T(8,128)(2,1)} collective-permute-done((bf16[750,1536]{1,0:T(8,128)(2,1)S(1)}, bf16[750,1536]{1,0:T(8,128)(2,1)}, u32[]{:S(2)}, u32[]{:S(2)}) %collective-permute-start) | collective-permute-done | bytes 2304032 | tf_op jit(solution)/shard_map/while/body/eval_jaxpr/ppermute | solution.py:10
  765.7 86.0 %conditional.15 = (bf16[750,1536]{1,0:T(8,128)(2,1)S(1)}) conditional(s32[]{:T(128)} %convert_element_type.146, bf16[750,1536]{1,0:T(8,128)(2,1)S(1)} %bitcast_select_fusion.5, (s32[]{:T(128)}, bf16[750,1536]{1,0:T(8,128)(2,1)S(1)}, f32[750]{0:T(1024)S(1)}, f32[2,1,1536]{2,1,0:T(1,128)S(1)}, bf16[1536,3072]{1,0:T(8,128)(2,1)}, ...), branch_computations={%region_1.1_spmd, %region_2.12_spmd} | conditional | flops 7183873536 | bytes 81529584 | solution.py:89
  765.7 85.9 %conditional.2 = (bf16[750,1536]{1,0:T(8,128)(2,1)S(1)}) conditional(s32[]{:T(128)} %convert_element_type.61, (bf16[750,1536]{1,0:T(8,128)(2,1)S(1)}, f32[750]{0:T(1024)S(1)}, f32[2,1,1536]{2,1,0:T(1,128)S(1)}, bf16[1536,3072]{1,0:T(8,128)(2,1)}, f32[2,1,31,1536]{3,2,1,0:T(8,128)S(1)}, /*index=5*/f32[2,1,1536]{2,1,0:T(1,128)S(1)}) %tuple.60, ...), branch_computations={%region_3.6_spmd, %region_8.11_spmd} | conditional | flops 7183873536 | bytes 81529472
  780.3 64.6 %fusion.164 = (f32[750]{0:T(1024)S(1)}, f32[750,1536]{1,0:T(8,128)}) fusion(f32[1536]{0:T(1024)S(1)} %get-tuple-element.595, f32[1536]{0:T(1024)S(1)} %get-tuple-element.596, f32[1536]{0:T(1024)S(1)} %get-tuple-element.597, f32[1536]{0:T(1024)S(1)} %get-tuple-element.598, f32[1536]{0:T(1024)S(1)} %get-tuple-element.599, f32[1536]{0:T(1024)S(1)} %get-tuple-element.600, ...), kind=kLoop, calls=%fused_computation.396 | loop fusion | flops 71423248 | bytes 9409464 | tf_op jit(solution)/shard_map/while/body/eval_jaxpr/cond/branch_1_fun/cond/branch_0_fun/reduce_sum | solution.py:14
  855.6 25.7 %collective-permute-done = bf16[750,1536]{1,0:T(8,128)(2,1)} collective-permute-done((bf16[750,1536]{1,0:T(8,128)(2,1)S(1)}, bf16[750,1536]{1,0:T(8,128)(2,1)}, u32[]{:S(2)}, u32[]{:S(2)}) %collective-permute-start) | collective-permute-done | bytes 2304032 | tf_op jit(solution)/shard_map/while/body/eval_jaxpr/ppermute | solution.py:10
  885.2 86.0 %conditional.15 = (bf16[750,1536]{1,0:T(8,128)(2,1)S(1)}) conditional(s32[]{:T(128)} %convert_element_type.146, bf16[750,1536]{1,0:T(8,128)(2,1)S(1)} %bitcast_select_fusion.5, (s32[]{:T(128)}, bf16[750,1536]{1,0:T(8,128)(2,1)S(1)}, f32[750]{0:T(1024)S(1)}, f32[2,1,1536]{2,1,0:T(1,128)S(1)}, bf16[1536,3072]{1,0:T(8,128)(2,1)}, ...), branch_computations={%region_1.1_spmd, %region_2.12_spmd} | conditional | flops 7183873536 | bytes 81529584 | solution.py:89
  885.2 86.0 %conditional.2 = (bf16[750,1536]{1,0:T(8,128)(2,1)S(1)}) conditional(s32[]{:T(128)} %convert_element_type.61, (bf16[750,1536]{1,0:T(8,128)(2,1)S(1)}, f32[750]{0:T(1024)S(1)}, f32[2,1,1536]{2,1,0:T(1,128)S(1)}, bf16[1536,3072]{1,0:T(8,128)(2,1)}, f32[2,1,31,1536]{3,2,1,0:T(8,128)S(1)}, /*index=5*/f32[2,1,1536]{2,1,0:T(1,128)S(1)}) %tuple.60, ...), branch_computations={%region_3.6_spmd, %region_8.11_spmd} | conditional | flops 7183873536 | bytes 81529472
  899.8 64.6 %fusion.164 = (f32[750]{0:T(1024)S(1)}, f32[750,1536]{1,0:T(8,128)}) fusion(f32[1536]{0:T(1024)S(1)} %get-tuple-element.595, f32[1536]{0:T(1024)S(1)} %get-tuple-element.596, f32[1536]{0:T(1024)S(1)} %get-tuple-element.597, f32[1536]{0:T(1024)S(1)} %get-tuple-element.598, f32[1536]{0:T(1024)S(1)} %get-tuple-element.599, f32[1536]{0:T(1024)S(1)} %get-tuple-element.600, ...), kind=kLoop, calls=%fused_computation.396 | loop fusion | flops 71423248 | bytes 9409464 | tf_op jit(solution)/shard_map/while/body/eval_jaxpr/cond/branch_1_fun/cond/branch_0_fun/reduce_sum | solution.py:14
  1000.4 90.1 %collective-permute-start = (bf16[750,1536]{1,0:T(8,128)(2,1)S(1)}, bf16[750,1536]{1,0:T(8,128)(2,1)}, u32[]{:S(2)}, u32[]{:S(2)}) collective-permute-start(bf16[750,1536]{1,0:T(8,128)(2,1)S(1)} %get-tuple-element.904), channel_id=1, source_target_pairs={{96,0},{0,32},{32,64},{64,96},{97,1},{1,33},{33,65},{65,97},{98,2}... | collective-permute-start | bytes 6912008 | tf_op jit(solution)/shard_map/while/body/eval_jaxpr/ppermute | solution.py:10
  1094.4 21.4 %collective-permute-done = bf16[750,1536]{1,0:T(8,128)(2,1)} collective-permute-done((bf16[750,1536]{1,0:T(8,128)(2,1)S(1)}, bf16[750,1536]{1,0:T(8,128)(2,1)}, u32[]{:S(2)}, u32[]{:S(2)}) %collective-permute-start) | collective-permute-done | bytes 2304032 | tf_op jit(solution)/shard_map/while/body/eval_jaxpr/ppermute | solution.py:10
  1154.1 121.0 %all_to_all.5 = bf16[2,750,4,384]{3,0,1,2:T(2,128)(2,1)S(1)} all-to-all(bf16[2,750,4,384]{3,0,1,2:T(2,128)(2,1)} %copy.21), channel_id=1, replica_groups=mesh['pipe'=4,'dp'=32] {'pipe'}, dimensions={2} | all-to-all | bytes 9216000 | tf_op jit(solution)/shard_map/all_to_all | solution.py:112
  (139 shorter events, 236.8 us)
Async XLA Ops:
  6.5 217.8 %all-gather.2.cloned.1.call-start = ((), (), s32[]{:S(2)}) async-start(), calls=%async_computation.1 | async-start | bytes 19464192 | tf_op jit(solution)/shard_map/all_gather | solution.py:101
  8.3 5.2 copy-start.9
  238.8 4.0 copy-start.6
  238.8 4.0 copy-start.7
  246.7 90.5 %collective-permute-start = (bf16[750,1536]{1,0:T(8,128)(2,1)S(1)}, bf16[750,1536]{1,0:T(8,128)(2,1)}, u32[]{:S(2)}, u32[]{:S(2)}) collective-permute-start(bf16[750,1536]{1,0:T(8,128)(2,1)S(1)} %get-tuple-element.904), channel_id=1, source_target_pairs={{96,0},{0,32},{32,64},{64,96},{97,1},{1,33},{33,65},{65,97},{98,2}... | collective-permute-start | bytes 6912008 | tf_op jit(solution)/shard_map/while/body/eval_jaxpr/ppermute | solution.py:10
  420.5 3.7 copy-start.1
  427.3 28.7 %collective-permute-start = (bf16[750,1536]{1,0:T(8,128)(2,1)S(1)}, bf16[750,1536]{1,0:T(8,128)(2,1)}, u32[]{:S(2)}, u32[]{:S(2)}) collective-permute-start(bf16[750,1536]{1,0:T(8,128)(2,1)S(1)} %get-tuple-element.904), channel_id=1, source_target_pairs={{96,0},{0,32},{32,64},{64,96},{97,1},{1,33},{33,65},{65,97},{98,2}... | collective-permute-start | bytes 6912008 | tf_op jit(solution)/shard_map/while/body/eval_jaxpr/ppermute | solution.py:10
  539.3 3.7 copy-start.1
  546.1 26.0 %collective-permute-start = (bf16[750,1536]{1,0:T(8,128)(2,1)S(1)}, bf16[750,1536]{1,0:T(8,128)(2,1)}, u32[]{:S(2)}, u32[]{:S(2)}) collective-permute-start(bf16[750,1536]{1,0:T(8,128)(2,1)S(1)} %get-tuple-element.904), channel_id=1, source_target_pairs={{96,0},{0,32},{32,64},{64,96},{97,1},{1,33},{33,65},{65,97},{98,2}... | collective-permute-start | bytes 6912008 | tf_op jit(solution)/shard_map/while/body/eval_jaxpr/ppermute | solution.py:10
  576.0 115.6 %collective-permute-start = (bf16[750,1536]{1,0:T(8,128)(2,1)S(1)}, bf16[750,1536]{1,0:T(8,128)(2,1)}, u32[]{:S(2)}, u32[]{:S(2)}) collective-permute-start(bf16[750,1536]{1,0:T(8,128)(2,1)S(1)} %get-tuple-element.904), channel_id=1, source_target_pairs={{96,0},{0,32},{32,64},{64,96},{97,1},{1,33},{33,65},{65,97},{98,2}... | collective-permute-start | bytes 6912008 | tf_op jit(solution)/shard_map/while/body/eval_jaxpr/ppermute | solution.py:10
  695.5 66.2 %collective-permute-start = (bf16[750,1536]{1,0:T(8,128)(2,1)S(1)}, bf16[750,1536]{1,0:T(8,128)(2,1)}, u32[]{:S(2)}, u32[]{:S(2)}) collective-permute-start(bf16[750,1536]{1,0:T(8,128)(2,1)S(1)} %get-tuple-element.904), channel_id=1, source_target_pairs={{96,0},{0,32},{32,64},{64,96},{97,1},{1,33},{33,65},{65,97},{98,2}... | collective-permute-start | bytes 6912008 | tf_op jit(solution)/shard_map/while/body/eval_jaxpr/ppermute | solution.py:10
  844.9 3.7 copy-start
  851.7 29.6 %collective-permute-start = (bf16[750,1536]{1,0:T(8,128)(2,1)S(1)}, bf16[750,1536]{1,0:T(8,128)(2,1)}, u32[]{:S(2)}, u32[]{:S(2)}) collective-permute-start(bf16[750,1536]{1,0:T(8,128)(2,1)S(1)} %get-tuple-element.904), channel_id=1, source_target_pairs={{96,0},{0,32},{32,64},{64,96},{97,1},{1,33},{33,65},{65,97},{98,2}... | collective-permute-start | bytes 6912008 | tf_op jit(solution)/shard_map/while/body/eval_jaxpr/ppermute | solution.py:10
  964.4 3.7 copy-start
  971.2 25.3 %collective-permute-start = (bf16[750,1536]{1,0:T(8,128)(2,1)S(1)}, bf16[750,1536]{1,0:T(8,128)(2,1)}, u32[]{:S(2)}, u32[]{:S(2)}) collective-permute-start(bf16[750,1536]{1,0:T(8,128)(2,1)S(1)} %get-tuple-element.904), channel_id=1, source_target_pairs={{96,0},{0,32},{32,64},{64,96},{97,1},{1,33},{33,65},{65,97},{98,2}... | collective-permute-start | bytes 6912008 | tf_op jit(solution)/shard_map/while/body/eval_jaxpr/ppermute | solution.py:10
  1000.4 115.4 %collective-permute-start = (bf16[750,1536]{1,0:T(8,128)(2,1)S(1)}, bf16[750,1536]{1,0:T(8,128)(2,1)}, u32[]{:S(2)}, u32[]{:S(2)}) collective-permute-start(bf16[750,1536]{1,0:T(8,128)(2,1)S(1)} %get-tuple-element.904), channel_id=1, source_target_pairs={{96,0},{0,32},{32,64},{64,96},{97,1},{1,33},{33,65},{65,97},{98,2}... | collective-permute-start | bytes 6912008 | tf_op jit(solution)/shard_map/while/body/eval_jaxpr/ppermute | solution.py:10
  1123.5 3.4 copy-start.2
  1126.9 2.0 copy-start.5
  1126.9 2.0 copy-start.8
Sparse Core Ops, SparseCore 0:
  9.0 215.3 all-gather.1
where the time goes:
time: 1290 us; the launch traced here: 1280 us
  waiting for transfers between devices  487 us (38%)
  other arithmetic  348 us (27%)
  starting transfers between devices  189 us (15%)
  blocking collectives  121 us (9%)
  local copies, waits for them, and re-layouts  73.8 us (6%)
  matrix products  40.3 us (3%)
  between operations  13.8 us (1%)
    ppermute x8, waiting for transfers between devices, passed_along(): return lax.ppermute(block, axis, route)  278 us
    reduce_sum x8, other arithmetic, layer_norm(): centred = values - jnp.mean(values, axis=-1, keepdims=True)  260 us
    all_gather x1, waiting for transfers between devices, on_device(): gathered = lax.all_gather(lift_weight, 'dp', axis=2, tiled=True)[:, 0]  209 us
    ppermute x8, starting transfers between devices, passed_along(): return lax.ppermute(block, axis, route)  189 us
    all_to_all x1, blocking collectives, on_device(): lax.all_to_all(pieces, 'pipe', split_axis=2, concat_axis=2, tiled=True)  121 us
    dot_general x4, matrix products, conv_module(): lifted = jnp.dot(normed, lift_weight, preferred_element_type=jnp.float32)  40.3 us
  transfers between devices with their start and end apart: 9, of which 9 were waited for; matrix products, arithmetic and copies ran while one was open for 3% of the time, Pallas kernels for 0%

commit v1 on v0

v1 whole, which is shorter than its diff:
```python
import functools

import jax
import jax.numpy as jnp
from jax import lax
from jax.experimental import pallas as pl
from jax.experimental.pallas import tpu as pltpu
from jax.sharding import PartitionSpec as P

ROWS = 512; SEG = ROWS // 8; D = 1536; TAPS = 31; HALF = 15; EPS = 1e-5
f32 = jnp.float32

def sigm(v):
    return 1.0 / (1.0 + jnp.exp(-v))

class Module:
    def __init__(s, st, mask, prm, wb, norm, gpad, mix):
        s.st, s.mask, s.prm, s.wb, s.norm, s.gpad, s.mix = st, mask, prm, wb, norm, gpad, mix
    def ln1(s, m):
        gain = s.prm[lax.rem(m, 4), lax.div(m, 4), TAPS:TAPS + 1, :]
        @pl.loop(0, ROWS // 16)
        def _(r):
            rows = pl.ds(pl.multiple_of(r * 16, 16), 16)
            v = s.st[rows, :].astype(f32)
            v = v - jnp.mean(v, axis=-1, keepdims=True)
            q = lax.rsqrt(jnp.mean(v * v, axis=-1, keepdims=True) + EPS)
            s.norm[rows, :] = (v * q * gain).astype(jnp.bfloat16)
    def cols(s, m, j):
        slot = lax.rem(m, 2)
        ca = pl.ds(pl.multiple_of(j * 256, 256), 256); cb = pl.ds(pl.multiple_of(D + j * 256, 256), 256)
        wa = s.wb[slot, :, :, :, :, ca].reshape(D, 256)
        a = jnp.dot(s.norm[...], wa, preferred_element_type=f32)
        wg = s.wb[slot, :, :, :, :, cb].reshape(D, 256)
        b = jnp.dot(s.norm[...], wg, preferred_element_type=f32)
        sub = lax.broadcasted_iota(jnp.int32, (HALF, 8, 128), 1)
        for q in range(2):
            l = slice(q * 128, q * 128 + 128)
            g = (a[:, l] * sigm(b[:, l]) * s.mask[...]).reshape(SEG, 8, 128)
            s.gpad[q, 16:16 + SEG] = g
            s.gpad[q, 1:16] = jnp.where(sub == 0, 0.0, pltpu.roll(g[SEG - HALF:], 1, 1))
            s.gpad[q, 16 + SEG:16 + SEG + HALF] = jnp.where(sub == 7, 0.0, pltpu.roll(g[:HALF], 7, 1))
        NB = 8
        for q in range(2):
            lanes = pl.ds(pl.multiple_of(j * 256 + q * 128, 128), 128)
            @pl.loop(0, SEG // NB)
            def _(rb):
                base = rb * NB
                w = [jnp.broadcast_to(s.prm[lax.rem(m, 4), lax.div(m, 4), k:k + 1, lanes], (8, 128)) for k in range(TAPS)]
                acc = [None] * NB
                for t in range(NB + TAPS - 1):
                    x = s.gpad[q, base + 1 + t]
                    for o in range(NB):
                        k = t - o
                        if 0 <= k < TAPS:
                            acc[o] = x * w[k] if acc[o] is None else acc[o] + x * w[k]
                for o in range(NB):
                    s.mix[base + o, :, lanes] = acc[o]
    def ln2(s, m):
        gain = s.prm[lax.rem(m, 4), lax.div(m, 4), TAPS + 1:TAPS + 2, :]
        @pl.loop(0, ROWS // 16)
        def _(r):
            rows = pl.ds(pl.multiple_of(r * 16, 16), 16)
            v = s.mix[pl.ds(pl.multiple_of(r * 2, 2), 2)].reshape(16, D)
            v = v - jnp.mean(v, axis=-1, keepdims=True)
            q = lax.rsqrt(jnp.mean(v * v, axis=-1, keepdims=True) + EPS)
            y = v * q * gain
            s.st[rows, :] = (s.st[rows, :].astype(f32) + s.mask[rows, :1] * (y * sigm(y))).astype(jnp.bfloat16)
    def run(s, m):
        s.ln1(m)
        @pl.loop(0, 6)
        def _(j): s.cols(m, j)
        s.ln2(m)


SPLIT = (4, 5, 3)
MESH = pl.DeviceIdType.MESH

def div(a, b): return lax.div(a, jnp.int32(b))

def rem(a, b): return lax.rem(a, jnp.int32(b))

def coords():
    pipe = lax.axis_index("pipe"); dp = lax.axis_index("dp")
    return rem(div(dp, 4), 4), rem(dp, 4), div(pipe, 2) * 2 + div(dp, 16), rem(pipe, 2)

def dev(x, y, z, core):
    return {"pipe": div(z, 2) * 2 + core, "dp": rem(z, 2) * 16 + x * 4 + y}

class Ring:
    def __init__(s, pos, at, unit, half, present, send, recv):
        s.pos, s.at, s.unit, s.half, s.present, s.send, s.recv = pos, at, unit, half, present, send, recv
    def copy(s, k, src, to):
        return pltpu.make_async_remote_copy(src, src, s.send.at[k], s.recv.at[k], device_id=s.at(to), device_id_type=MESH)
    def sends(s):
        p = s.pos; up, dn = rem(p + 1, 4), rem(p + 3, 4)
        return [(s.present(p), lambda: s.copy(0, s.unit(p), up)), (s.present(p), lambda: s.copy(1, s.unit(p), dn)),
                (s.present(dn), lambda: s.copy(2, s.half(dn, 0), up)), (s.present(up), lambda: s.copy(3, s.half(up, 1), dn))]
    def recvs(s):
        p = s.pos; up, dn, op = rem(p + 1, 4), rem(p + 3, 4), rem(p + 2, 4)
        return [(s.present(dn), lambda: s.copy(0, s.unit(dn), up)), (s.present(up), lambda: s.copy(1, s.unit(up), dn)),
                (s.present(op), lambda: s.copy(2, s.half(op, 0), up)), (s.present(op), lambda: s.copy(3, s.half(op, 1), dn))]

def do(item, what):
    cond, mk = item
    if cond is True:
        getattr(mk(), what)()
    else:
        @pl.when(cond)
        def _(): getattr(mk(), what)()

class Gather:
    def __init__(s, w_ref, full, sems):
        s.w, s.full = w_ref, full
        s.x, s.y, s.z, s.core = coords()
        s.zl, s.zh = rem(s.z, 2), div(s.z, 2)
        s.sec = s.zh * 2 + s.core
        (s.own_sem, s.zs, s.zr, s.cs, s.cr, s.ms, s.mr, s.fs, s.fr, s.ds, s.dr) = sems
    def cols(s, part, n=1, core=None):
        core = s.core if core is None else core
        return pl.ds(pl.multiple_of(core * 1536 + 128 * sum(SPLIT[:part]), 128), 128 * sum(SPLIT[part:part + n]))
    def peers(s):
        x, y, z, c = s.x, s.y, s.z, s.core
        r = [dev(x, y, z, 1 - c)]
        r += [dev(rem(x + d, 4), y, z, c) for d in (1, 2, 3)]
        r += [dev(x, rem(y + d, 4), z, c) for d in (1, 3)]
        r += [dev(x, y, rem(z + d, 4), c) for d in (1, 2, 3)]
        r += [dev(x, y, rem(z + 2, 4), 1 - c)]
        return r
    def own_copies(s):
        o = 1 - s.core
        mine, other = s.cols(0, 3), s.cols(0, 3, o)
        here = s.full.at[:, s.sec, s.zl, s.x, s.y]
        return (pltpu.make_async_copy(s.w.at[:, :, mine], here.at[:, :, mine], s.own_sem.at[0]),
                pltpu.make_async_remote_copy(s.w.at[:, :, other], here.at[:, :, other], s.own_sem.at[1], s.own_sem.at[2], device_id=dev(s.x, s.y, s.z, o), device_id_type=MESH))
    def own_arrival(s):
        mine = s.cols(0, 3)
        there = s.full.at[:, s.zh * 2 + 1 - s.core, s.zl, s.x, s.y]
        return pltpu.make_async_remote_copy(s.w.at[:, :, mine], there.at[:, :, mine], s.own_sem.at[1], s.own_sem.at[2], device_id=dev(s.x, s.y, s.z, 1 - s.core), device_id_type=MESH)
    def begin(s):
        a, b = s.own_copies()
        a.start(); b.start(); a.wait(); b.wait_send(); s.own_arrival().wait_recv()
    def mod(s, c):
        return s.full.at[div(c, 4), rem(c, 4)]
    def src(s, c):
        return s.zh == div(rem(c, 4), 2)
    def first_sends(s, c):
        W = s.mod(c); out = []
        for d in (1, 2, 3):
            out.append((s.src(c), functools.partial(s.zcopy, W, c, s.zl, d - 1, rem(s.z + d, 4))))
        for d in (1, 2, 3):
            out.append((s.src(c), functools.partial(s.ccopy, W, c, s.x, d - 1, rem(s.x + d, 4))))
        return out
    def zcopy(s, W, c, zl, k, to):
        sl = W.at[zl, s.x, s.y, :, s.cols(0, 2)]
        return pltpu.make_async_remote_copy(sl, sl, s.zs.at[c, k], s.zr.at[c, zl], device_id=dev(s.x, s.y, to, s.core), device_id_type=MESH)
    def ccopy(s, W, c, q, k, to):
        sl = W.at[s.zl, q, s.y, :, s.cols(2)]
        return pltpu.make_async_remote_copy(sl, sl, s.cs.at[c, k], s.cr.at[c, k], device_id=dev(to, s.y, s.z, s.core), device_id_type=MESH)
    def first_recvs(s, c):
        W = s.mod(c); out = []
        for zl in (0, 1):
            out.append((jnp.logical_not(jnp.logical_and(s.src(c), s.zl == zl)), functools.partial(s.zcopy, W, c, zl, 0, s.z)))
        for d in (1, 2, 3):
            out.append((s.src(c), functools.partial(s.ccopy, W, c, rem(s.x + 4 - d, 4), d - 1, s.x)))
        return out
    def mids(s, c):
        W = s.mod(c); yes = lambda q: True; src = lambda q: s.src(c)
        a, b, cc = s.cols(0), s.cols(1), s.cols(2)
        atx = lambda q: dev(q, s.y, s.z, s.core)
        aty = lambda q: dev(s.x, q, s.z, s.core)
        return [Ring(s.x, atx, lambda q: W.at[:, q, s.y, :, a], lambda q, h: W.at[h, q, s.y, :, a], yes, s.ms.at[c, 0], s.mr.at[c, 0]),
                Ring(s.y, aty, lambda q: W.at[:, s.x, q, :, b], lambda q, h: W.at[h, s.x, q, :, b], yes, s.ms.at[c, 1], s.mr.at[c, 1]),
                Ring(s.y, aty, lambda q: W.at[s.zl, :, q, :, cc], lambda q, h: W.at[s.zl, pl.ds(2 * h, 2), q, :, cc], src, s.ms.at[c, 2], s.mr.at[c, 2])]
    def fins(s, c):
        W = s.mod(c); yes = lambda q: True
        a, b, cc = s.cols(0), s.cols(1), s.cols(2)
        atx = lambda q: dev(q, s.y, s.z, s.core)
        aty = lambda q: dev(s.x, q, s.z, s.core)
        atz = lambda q: dev(s.x, s.y, q, s.core)
        return [Ring(s.y, aty, lambda q: W.at[:, :, q, :, a], lambda q, h: W.at[h, :, q, :, a], yes, s.fs.at[c, 0], s.fr.at[c, 0]),
                Ring(s.x, atx, lambda q: W.at[:, q, :, :, b], lambda q, h: W.at[h, q, :, :, b], yes, s.fs.at[c, 1], s.fr.at[c, 1]),
                Ring(s.z, atz, lambda q: W.at[rem(q, 2), :, :, :, cc], lambda q, h: W.at[rem(q, 2), pl.ds(2 * h, 2), :, :, cc],
                     lambda q: div(q, 2) == div(rem(c, 4), 2), s.fs.at[c, 2], s.fr.at[c, 2])]
    def swap(s, c, part, core):
        sl = s.mod(c).at[:, :, :, :, s.cols(part, 1, core)]
        return pltpu.make_async_remote_copy(sl, sl, s.ds.at[c, part], s.dr.at[c, part], device_id=dev(s.x, s.y, s.z, 1 - s.core), device_id_type=MESH)
    def e1(s, c):
        for it in s.first_sends(c): do(it, "start")
    def e2(s, c):
        for it in s.first_recvs(c): do(it, "wait_recv")
        for r in s.mids(c):
            for it in r.sends()[:2]: do(it, "start")
    def relay(s, rings):
        for k in (0, 1):
            for r in rings:
                do(r.recvs()[k], "wait_recv"); do(r.sends()[2 + k], "start")
    def e3(s, c): s.relay(s.mids(c))
    def e4(s, c):
        for r, f in zip(s.mids(c), s.fins(c)):
            for it in r.recvs()[2:]: do(it, "wait_recv")
            for it in f.sends()[:2]: do(it, "start")
    def e5a(s, c): s.relay(s.fins(c))
    def e5b(s, c):
        for p, r in enumerate(s.fins(c)):
            for it in r.recvs()[2:]: do(it, "wait_recv")
            s.swap(c, p, s.core).start()
    def e6(s, c):
        for p in range(3): s.swap(c, p, 1 - s.core).wait_recv()
    def drain(s, c):
        for it in s.first_sends(c): do(it, "wait_send")
        for r in s.mids(c) + s.fins(c):
            for it in r.sends(): do(it, "wait_send")
        for p in range(3): s.swap(c, p, s.core).wait_send()


NG = 5

def guard(m, fn):
    @pl.when(jnp.logical_and(m >= 0, m < 8))
    def _(): fn(m)

class Shares:
    def __init__(s, g, send, recv, own):
        s.g, s.send, s.recv, s.own = g, send, recv, own
    def at(s, pipe):
        return {"pipe": pipe}
    def each(s, src_of, dst_of, what):
        me = s.g.sec
        for q in range(4):
            if what == "start":
                @pl.when(me != q)
                def _(): pltpu.make_async_remote_copy(src_of(q), dst_of(me), s.send.at[q], s.recv.at[me], device_id={"pipe": q}, device_id_type=MESH).start()
                @pl.when(me == q)
                def _(): pltpu.make_async_copy(src_of(q), dst_of(me), s.own).start()
            else:
                @pl.when(me != q)
                def _():
                    pltpu.make_async_remote_copy(src_of(q), dst_of(me), s.send.at[q], s.recv.at[me], device_id={"pipe": q}, device_id_type=MESH).wait_send()
                    pltpu.make_async_remote_copy(src_of(q), dst_of(q), s.send.at[q], s.recv.at[q], device_id={"pipe": q}, device_id_type=MESH).wait_recv()
                @pl.when(me == q)
                def _(): pltpu.make_async_copy(src_of(q), dst_of(me), s.own).wait()

def kernel(x_ref, mask_ref, prm_ref, w_ref, out_ref, full, st, wb, norm, gpad, mix, wsem, prm, ps, pr, po, os_, or_, oo, *sems):
    g = Gather(w_ref, full, sems)
    b = pltpu.get_barrier_semaphore()
    for d in g.peers():
        pl.semaphore_signal(b, inc=1, device_id=d, device_id_type=MESH)
    pl.semaphore_wait(b, len(g.peers()))
    shares = Shares(g, ps, pr, po)
    psrc, pdst = (lambda q: prm_ref), (lambda q: prm.at[q])
    g.begin()
    g.e1(jnp.int32(0))
    shares.each(psrc, pdst, "start")
    st[...] = x_ref[...]
    md = Module(st, mask_ref, prm, wb, norm, gpad, mix)
    load = lambda m: pltpu.make_async_copy(full.at[div(m, 4), rem(m, 4)], wb.at[rem(m, 2)], wsem.at[rem(m, 2)])
    def head(m):
        g.e6(m); load(m).start()
        @pl.when(m == 0)
        def _(): shares.each(psrc, pdst, "wait")
        md.ln1(m)
    def some(m, lo, hi):
        @pl.loop(lo, hi)
        def _(j): md.cols(m, j)
    @pl.loop(0, 14)
    def _(i):
        m = i - 6
        guard(m, head)
        @pl.when(i > 0)
        def _(): guard(i, g.e1)
        guard(i - 1, g.e2)
        guard(m, lambda m: load(m).wait())
        guard(m, lambda m: some(m, 0, 2))
        guard(i - 2, g.e3)
        guard(m, lambda m: some(m, 2, 3))
        guard(i - 3, g.e4)
        guard(m, lambda m: some(m, 3, 5))
        guard(i - 4, g.e5a)
        guard(m, lambda m: some(m, 5, 6))
        guard(m, md.ln2)
        guard(i - 5, g.e5b)
    outs = Shares(g, os_, or_, oo)
    osrc, odst = (lambda q: st.at[:, pl.ds(q * (D // 4), D // 4)]), (lambda q: out_ref.at[q])
    outs.each(osrc, odst, "start")
    @pl.loop(0, 8)
    def _(i): g.drain(i)
    outs.each(osrc, odst, "wait")

SEM = pltpu.SemaphoreType.DMA
V = pltpu.VMEM

def run(x, mask, prm, w):
    vm, hbm = pl.BlockSpec(memory_space=pltpu.VMEM), pl.BlockSpec(memory_space=pl.ANY)
    return pl.pallas_call(
        kernel,
        out_shape=(jax.ShapeDtypeStruct((4, ROWS, D // 4), jnp.bfloat16), jax.ShapeDtypeStruct((2, 4, 2, 4, 4, 48, 2 * D), jnp.bfloat16)),
        in_specs=[vm, vm, vm, vm],
        out_specs=(hbm, hbm),
        scratch_shapes=[
            V((ROWS, D), jnp.bfloat16), V((2, 2, 4, 4, 48, 2 * D), jnp.bfloat16), V((ROWS, D), jnp.bfloat16),
            V((2, 16 + SEG + 16, 8, 128), f32), V((SEG, 8, D), f32), SEM((2,)), V((4, 2, 40, D), f32),
            SEM((4,)), SEM((4,)), SEM, SEM((4,)), SEM((4,)), SEM,
            SEM((3,)), SEM((8, 3)), SEM((8, 2)), SEM((8, 3)), SEM((8, 3)), SEM((8, 3, 4)), SEM((8, 3, 4)), SEM((8, 3, 4)), SEM((8, 3, 4)), SEM((8, 3)), SEM((8, 3)),
        ],
        compiler_params=pltpu.CompilerParams(collective_id=0, has_side_effects=True, vmem_limit_bytes=60 * 2**20),
    )(x, mask, prm, w)[0]

def on_device(frames_in, lengths, norm_gain, lift_weight, depth_kernel, out_gain):
    frames = frames_in.shape[1]
    pipe = lax.axis_index("pipe")
    clip, half = pipe // 2, pipe % 2
    late = frames - ROWS
    p = jnp.arange(ROWS, dtype=jnp.int32)
    local = p % 8 * SEG + p // 8
    when = local + half * late
    pick = (when[:, None] == jnp.arange(frames, dtype=jnp.int32)[None]).astype(jnp.bfloat16)
    mine = lax.dynamic_index_in_dim(frames_in, clip, 0, keepdims=False)
    x = jnp.dot(pick, mine, preferred_element_type=f32).astype(jnp.bfloat16)
    length = lax.dynamic_index_in_dim(lengths, clip, 0, keepdims=False)
    mask = jnp.broadcast_to((when < length).astype(f32)[:, None], (ROWS, 128))
    prm = jnp.concatenate([depth_kernel[:, 0], norm_gain, out_gain, jnp.zeros((2, 7, D), f32)], axis=1)
    got = run(x, mask, prm, lift_weight[:, 0])
    t = jnp.arange(frames, dtype=jnp.int32)
    cut = frames // 2
    source = jnp.where(t < cut, local_row(t), ROWS + local_row(t - late))
    back = (source[:, None] == jnp.arange(2 * ROWS, dtype=jnp.int32)[None]).astype(jnp.bfloat16)
    got = got.reshape(2, 2 * ROWS, D // 4)
    return jnp.stack([jnp.dot(back, got[c], preferred_element_type=f32).astype(jnp.bfloat16) for c in range(2)])

def local_row(t):
    return t % SEG * 8 + t // SEG

def solution(mesh):
    return jax.shard_map(
        on_device,
        mesh=mesh,
        in_specs=(P("dp", None, None), P("dp"), P(None, "pipe", None), P(None, "pipe", "dp", None), P(None, "pipe", None, None), P(None, "pipe", None)),
        out_specs=P("dp", None, "pipe"),
        check_vma=False,
    )
```

time: 1290 us -> 426 us (0.33)
  waiting for transfers between devices: 487 us -> 0 us
  Pallas kernels: 0 us -> 402 us
  other arithmetic: 348 us -> 1.69 us
  starting transfers between devices: 189 us -> 0 us
  blocking collectives: 121 us -> 0 us
  local copies, waits for them, and re-layouts: 73.8 us -> 14.1 us
  matrix products: 40.3 us -> 7 us
  between operations: 13.8 us -> 0.08 us
    pallas_call x0 -> x1, Pallas kernels: none -> 402 us  [run(): pl.pallas_call(kernel, out_shape=(jax.ShapeDtypeStruct((4, ROWS, D // 4),...]
    ppermute x8 -> x0, waiting for transfers between devices: 278 us -> none  [passed_along(): return lax.ppermute(block, axis, route)]
    reduce_sum x16 -> x0, other arithmetic: 275 us -> none  [the longest x8 260 us: layer_norm(): centred = values - jnp.mean(values, axis=-1, keepdims=True)]
    all_gather x1 -> x0, waiting for transfers between devices: 209 us -> none  [on_device(): gathered = lax.all_gather(lift_weight, 'dp', axis=2, tiled=True)[:, 0]]
    ppermute x8 -> x0, starting transfers between devices: 189 us -> none  [passed_along(): return lax.ppermute(block, axis, route)]
    all_to_all x1 -> x0, blocking collectives: 121 us -> none  [on_device(): lax.all_to_all(pieces, 'pipe', split_axis=2, concat_axis=2, tiled=True)]
    dot_general x4 -> x3, matrix products: 40.3 us -> 7 us  [the longest x1 4.98 us: on_device(): x = jnp.dot(pick, mine, preferred_element_type=f32).astype(jnp.bfloat16)]
    select_n x9 -> x1, other arithmetic: 22.7 us -> 0.02 us  [on_device(): source = jnp.where(t < cut, local_row(t), ROWS + local_row(t - late))]
  transfers between devices with their start and end apart: 9 -> 0, of which waited for: 9 -> 0; matrix products, arithmetic and copies ran while one was open for 3% -> 0% of each run, Pallas kernels for 0% -> 0%
where the time goes in v1:
time: 426 us; the launch traced here: 425 us
  Pallas kernels  402 us (94%)
  local copies, waits for them, and re-layouts  14.1 us (3%)
  matrix products  7 us (2%)
    pallas_call x1, Pallas kernels, run(): pl.pallas_call(kernel, out_shape=(jax.ShapeDtypeStruct((4, ROWS, D // 4),...  402 us
    dynamic_slice x1, local copies, waits for them, and re-layouts, on_device(): mine = lax.dynamic_index_in_dim(frames_in, clip, 0, keepdims=False)  9.12 us

profile of v1, /device:TPU:1, one launch (start us, length us, event | category | flops | bytes accessed | tf_op | source)
XLA Modules:
  0.0 425.2 jit_solution(12996427953942336668)
XLA Ops:
  0.0 9.1 %constant_dynamic-slice_fusion = bf16[1,750,1536]{2,0,1:T(2,128)(2,1)} fusion(bf16[2,750,1536]{2,0,1:T(2,128)(2,1)} %param.6, s32[]{:T(128)S(6)} %select_n.102), kind=kLoop, calls=%fused_computation.62 | loop fusion | bytes 4608004 | tf_op jit(solution)/shard_map/jit(dynamic_index_in_dim)/dynamic_slice | solution.py:317
  9.1 0.0 copy-start.3
  9.1 0.0 copy-start
  9.1 0.0 copy-start.1
  9.1 0.0 copy-start.2
  9.2 5.0 %convolution_convert_fusion.x_ref = bf16[512,1536]{1,0:T(8,128)(2,1)} fusion(bf16[1,750,1536]{2,0,1:T(2,128)(2,1)} %constant_dynamic-slice_fusion, s32[512]{0:T(512)S(1)} %fusion.35), kind=kOutput, calls=%fused_computation.3 | convolution fusion | flops 1180818432 | bytes 3878912 | tf_op jit(solution)/shard_map/dot_general | solution.py:318
  14.1 0.0 copy-done.3
  14.1 0.6 dynamic_slice.9
  14.7 0.7 compare_convert_fusion
  15.4 0.8 broadcast_in_dim.4.mask_ref
  16.2 0.0 copy-done
  16.3 0.1 pad.5.clone
  16.3 0.0 copy-done.1
  16.3 0.0 copy-done.2
  16.3 0.9 maximum_maximum_fusion.prm_ref
  17.2 402.3 %shard_map.64 = (bf16[4,512,384]{2,1,0:T(8,128)(2,1)}, bf16[2,4,2,4,4,48,3072]{6,5,4,3,2,1,0:T(8,128)(2,1)}) custom-call(bf16[512,1536]{1,0:T(8,128)(2,1)} %convolution_convert_fusion.x_ref, f32[512,128]{1,0:T(8,128)} %broadcast_in_dim.4.mask_ref, f32[2,40,1536]{2,1,0:T(8,128)} %maximum_maximum_fusion.prm_ref, bf16[2,48,3072]{2,1,0:T(8,128)(2,1)} %bitcast.19), custom_call_target="tpu_custom_call" | custom-call | tf_op jit(solution)/shard_map/pallas_call | solution.py:294
  419.5 1.5 fusion.40
  421.1 1.0 fusion.6
  422.1 1.0 fusion.7
  423.1 0.1 pad_maximum_fusion
  423.3 1.9 copy.9
  (4 shorter events, 0.1 us)
Async XLA Ops:
  9.1 5.0 %copy-start.3 = (s32[2]{0:T(128)S(1)}, s32[2]{0:T(128)}, u32[]{:S(2)}) copy-start(s32[2]{0:T(128)} %param.7) | copy-start | bytes 28
  9.1 7.1 %copy-start = (f32[2,1,31,1536]{3,1,2,0:T(1,128)S(1)}, f32[2,1,31,1536]{3,1,2,0:T(1,128)}, u32[]{:S(2)}) copy-start(f32[2,1,31,1536]{3,1,2,0:T(1,128)} %param.10) | copy-start | bytes 1142788
  9.1 7.2 %copy-start.1 = (f32[2,1,1536]{2,1,0:T(1,128)S(1)}, f32[2,1,1536]{2,1,0:T(1,128)}, u32[]{:S(2)}) copy-start(f32[2,1,1536]{2,1,0:T(1,128)} %param.11) | copy-start | bytes 36868
  9.1 7.2 %copy-start.2 = (f32[2,1,1536]{2,1,0:T(1,128)S(1)}, f32[2,1,1536]{2,1,0:T(1,128)}, u32[]{:S(2)}) copy-start(f32[2,1,1536]{2,1,0:T(1,128)} %param.8) | copy-start | bytes 36868

commit v2 on v1

--- a/solution.py
+++ b/solution.py
@@ -7,68 +7,79 @@
 from jax.experimental.pallas import tpu as pltpu
 from jax.sharding import PartitionSpec as P
 
-ROWS = 512; SEG = ROWS // 8; D = 1536; TAPS = 31; HALF = 15; EPS = 1e-5
+ROWS = 512; LANES = 16; SEG = ROWS // LANES; D = 1536; TAPS = 31; HALF = 15; EPS = 1e-5
 f32 = jnp.float32
+bf16 = jnp.bfloat16
+GROUP, NB = 8, 8
 
 def sigm(v):
     return 1.0 / (1.0 + jnp.exp(-v))
 
 class Module:
-    def __init__(s, st, mask, prm, wb, norm, gpad, mix):
-        s.st, s.mask, s.prm, s.wb, s.norm, s.gpad, s.mix = st, mask, prm, wb, norm, gpad, mix
+    def __init__(s, st, mask, prm, wb, norm, gpads, mix):
+        s.st, s.mask, s.prm, s.wb, s.norm, s.gpads, s.mix = st, mask, prm, wb, norm, gpads, mix
+    def par(s, m, row, n=1):
+        return s.prm.at[lax.rem(m, jnp.int32(4)), lax.div(m, jnp.int32(4)), row:row + n]
     def ln1(s, m):
-        gain = s.prm[lax.rem(m, 4), lax.div(m, 4), TAPS:TAPS + 1, :]
-        @pl.loop(0, ROWS // 16)
+        gain = s.par(m, TAPS)[...]
+        @pl.loop(0, ROWS // 32)
         def _(r):
-            rows = pl.ds(pl.multiple_of(r * 16, 16), 16)
-            v = s.st[rows, :].astype(f32)
-            v = v - jnp.mean(v, axis=-1, keepdims=True)
-            q = lax.rsqrt(jnp.mean(v * v, axis=-1, keepdims=True) + EPS)
-            s.norm[rows, :] = (v * q * gain).astype(jnp.bfloat16)
-    def cols(s, m, j):
-        slot = lax.rem(m, 2)
-        ca = pl.ds(pl.multiple_of(j * 256, 256), 256); cb = pl.ds(pl.multiple_of(D + j * 256, 256), 256)
-        wa = s.wb[slot, :, :, :, :, ca].reshape(D, 256)
-        a = jnp.dot(s.norm[...], wa, preferred_element_type=f32)
-        wg = s.wb[slot, :, :, :, :, cb].reshape(D, 256)
-        b = jnp.dot(s.norm[...], wg, preferred_element_type=f32)
-        sub = lax.broadcasted_iota(jnp.int32, (HALF, 8, 128), 1)
+            for h in range(2):
+                rows = pl.ds(pl.multiple_of(r * 32 + h * 16, 16), 16)
+                v = s.st[rows, :].astype(f32)
+                v = v - jnp.mean(v, axis=-1, keepdims=True)
+                q = lax.rsqrt(jnp.mean(v * v, axis=-1, keepdims=True) + EPS) * s.mask[rows, :1]
+                s.norm[rows, :] = (v * q * gain).astype(bf16)
+    def lift(s, m, j):
+        slot = lax.rem(m, jnp.int32(2)); pad = s.gpads[j % 2]
+        w = lambda c: s.wb[slot, :, :, :, :, c:c + 256].reshape(D, 256)
+        a = jnp.dot(s.norm[...], w(j * 256), preferred_element_type=f32)
+        b = jnp.dot(s.norm[...], w(D + j * 256), preferred_element_type=f32)
+        sub = lax.broadcasted_iota(jnp.int32, (HALF, LANES, 128), 1)
         for q in range(2):
             l = slice(q * 128, q * 128 + 128)
-            g = (a[:, l] * sigm(b[:, l]) * s.mask[...]).reshape(SEG, 8, 128)
-            s.gpad[q, 16:16 + SEG] = g
-            s.gpad[q, 1:16] = jnp.where(sub == 0, 0.0, pltpu.roll(g[SEG - HALF:], 1, 1))
-            s.gpad[q, 16 + SEG:16 + SEG + HALF] = jnp.where(sub == 7, 0.0, pltpu.roll(g[:HALF], 7, 1))
-        NB = 8
+            g = (a[:, l] * sigm(b[:, l])).reshape(SEG, LANES, 128)
+            pad[q, 16:16 + SEG] = g
+            pad[q, 1:16] = jnp.where(sub == 0, 0.0, pltpu.roll(g[SEG - HALF:], 1, 1))
+            pad[q, 16 + SEG:31 + SEG] = jnp.where(sub == LANES - 1, 0.0, pltpu.roll(g[:HALF], LANES - 1, 1))
+    def conv(s, m, j):
+        pad = s.gpads[j % 2]
         for q in range(2):
-            lanes = pl.ds(pl.multiple_of(j * 256 + q * 128, 128), 128)
-            @pl.loop(0, SEG // NB)
-            def _(rb):
-                base = rb * NB
-                w = [jnp.broadcast_to(s.prm[lax.rem(m, 4), lax.div(m, 4), k:k + 1, lanes], (8, 128)) for k in range(TAPS)]
+            c = slice(j * 256 + q * 128, j * 256 + q * 128 + 128)
+            taps = s.par(m, 0, 32)
+            w = [jnp.broadcast_to(taps[k:k + 1, c], (LANES, 128)).astype(bf16) for k in range(TAPS)]
+            for base in range(0, SEG, NB):
                 acc = [None] * NB
-                for t in range(NB + TAPS - 1):
-                    x = s.gpad[q, base + 1 + t]
+                x = {}
+                for k0 in range(0, TAPS, GROUP):
+                    ks = range(k0, min(TAPS, k0 + GROUP))
+                    for t in range(k0, k0 + len(ks) + NB - 1):
+                        if t not in x: x[t] = pad[q, base + 1 + t].astype(bf16)
                     for o in range(NB):
-                        k = t - o
-                        if 0 <= k < TAPS:
-                            acc[o] = x * w[k] if acc[o] is None else acc[o] + x * w[k]
+                        p = None
+                        for k in ks:
+                            p = x[o + k] * w[k] if p is None else p + x[o + k] * w[k]
+                        p = p.astype(f32)
+                        acc[o] = p if acc[o] is None else acc[o] + p
                 for o in range(NB):
-                    s.mix[base + o, :, lanes] = acc[o]
+                    s.mix[base + o, :, c] = acc[o]
     def ln2(s, m):
-        gain = s.prm[lax.rem(m, 4), lax.div(m, 4), TAPS + 1:TAPS + 2, :]
-        @pl.loop(0, ROWS // 16)
+        gain = s.par(m, TAPS + 1)[...]
+        @pl.loop(0, ROWS // 32)
         def _(r):
-            rows = pl.ds(pl.multiple_of(r * 16, 16), 16)
-            v = s.mix[pl.ds(pl.multiple_of(r * 2, 2), 2)].reshape(16, D)
-            v = v - jnp.mean(v, axis=-1, keepdims=True)
-            q = lax.rsqrt(jnp.mean(v * v, axis=-1, keepdims=True) + EPS)
-            y = v * q * gain
-            s.st[rows, :] = (s.st[rows, :].astype(f32) + s.mask[rows, :1] * (y * sigm(y))).astype(jnp.bfloat16)
+            for h in range(2):
+                rows = pl.ds(pl.multiple_of(r * 32 + h * 16, 16), 16)
+                v = s.mix[r * 2 + h]
+                v = v - jnp.mean(v, axis=-1, keepdims=True)
+                q = lax.rsqrt(jnp.mean(v * v, axis=-1, keepdims=True) + EPS)
+                y = v * q * gain
+                s.st[rows, :] = (s.st[rows, :].astype(f32) + s.mask[rows, :1] * (y * sigm(y))).astype(bf16)
+    def stage(s, m, j):
+        if j > 0: s.conv(m, j - 1)
+        if j < 6: s.lift(m, j)
     def run(s, m):
         s.ln1(m)
-        @pl.loop(0, 6)
-        def _(j): s.cols(m, j)
+        for j in range(7): s.stage(m, j)
         s.ln2(m)
 
 
@@ -213,8 +224,6 @@
         for p in range(3): s.swap(c, p, s.core).wait_send()
 
 
-NG = 5
-
 def guard(m, fn):
     @pl.when(jnp.logical_and(m >= 0, m < 8))
     def _(): fn(m)
@@ -240,7 +249,7 @@
                 @pl.when(me == q)
                 def _(): pltpu.make_async_copy(src_of(q), dst_of(me), s.own).wait()
 
-def kernel(x_ref, mask_ref, prm_ref, w_ref, out_ref, full, st, wb, norm, gpad, mix, wsem, prm, ps, pr, po, os_, or_, oo, *sems):
+def kernel(x_ref, mask_ref, prm_ref, w_ref, out_ref, full, st, wb, norm, gpa, gpb, mix, wsem, prm, ps, pr, po, os_, or_, oo, *sems):
     g = Gather(w_ref, full, sems)
     b = pltpu.get_barrier_semaphore()
     for d in g.peers():
@@ -252,7 +261,7 @@
     g.e1(jnp.int32(0))
     shares.each(psrc, pdst, "start")
     st[...] = x_ref[...]
-    md = Module(st, mask_ref, prm, wb, norm, gpad, mix)
+    md = Module(st, mask_ref, prm, wb, norm, (gpa, gpb), mix)
     load = lambda m: pltpu.make_async_copy(full.at[div(m, 4), rem(m, 4)], wb.at[rem(m, 2)], wsem.at[rem(m, 2)])
     def head(m):
         g.e6(m); load(m).start()
@@ -260,8 +269,7 @@
         def _(): shares.each(psrc, pdst, "wait")
         md.ln1(m)
     def some(m, lo, hi):
-        @pl.loop(lo, hi)
-        def _(j): md.cols(m, j)
+        for j in range(lo, hi): md.stage(m, j)
     @pl.loop(0, 14)
     def _(i):
         m = i - 6
@@ -272,11 +280,11 @@
         guard(m, lambda m: load(m).wait())
         guard(m, lambda m: some(m, 0, 2))
         guard(i - 2, g.e3)
-        guard(m, lambda m: some(m, 2, 3))
+        guard(m, lambda m: some(m, 2, 4))
         guard(i - 3, g.e4)
-        guard(m, lambda m: some(m, 3, 5))
+        guard(m, lambda m: some(m, 4, 5))
         guard(i - 4, g.e5a)
-        guard(m, lambda m: some(m, 5, 6))
+        guard(m, lambda m: some(m, 5, 7))
         guard(m, md.ln2)
         guard(i - 5, g.e5b)
     outs = Shares(g, os_, or_, oo)
@@ -298,7 +306,7 @@
         out_specs=(hbm, hbm),
         scratch_shapes=[
             V((ROWS, D), jnp.bfloat16), V((2, 2, 4, 4, 48, 2 * D), jnp.bfloat16), V((ROWS, D), jnp.bfloat16),
-            V((2, 16 + SEG + 16, 8, 128), f32), V((SEG, 8, D), f32), SEM((2,)), V((4, 2, 40, D), f32),
+            V((2, 32 + SEG, LANES, 128), f32), V((2, 32 + SEG, LANES, 128), f32), V((SEG, LANES, D), f32), SEM((2,)), V((4, 2, 40, D), f32),
             SEM((4,)), SEM((4,)), SEM, SEM((4,)), SEM((4,)), SEM,
             SEM((3,)), SEM((8, 3)), SEM((8, 2)), SEM((8, 3)), SEM((8, 3)), SEM((8, 3, 4)), SEM((8, 3, 4)), SEM((8, 3, 4)), SEM((8, 3, 4)), SEM((8, 3)), SEM((8, 3)),
         ],
@@ -311,7 +319,7 @@
     clip, half = pipe // 2, pipe % 2
     late = frames - ROWS
     p = jnp.arange(ROWS, dtype=jnp.int32)
-    local = p % 8 * SEG + p // 8
+    local = p % LANES * SEG + p // LANES
     when = local + half * late
     pick = (when[:, None] == jnp.arange(frames, dtype=jnp.int32)[None]).astype(jnp.bfloat16)
     mine = lax.dynamic_index_in_dim(frames_in, clip, 0, keepdims=False)
@@ -328,7 +336,7 @@
     return jnp.stack([jnp.dot(back, got[c], preferred_element_type=f32).astype(jnp.bfloat16) for c in range(2)])
 
 def local_row(t):
-    return t % SEG * 8 + t // SEG
+    return t % SEG * LANES + t // SEG
 
 def solution(mesh):
     return jax.shard_map(

time: 426 us -> 354 us (0.83)
  Pallas kernels: 402 us -> 331 us
    pallas_call x1, Pallas kernels: 402 us -> 331 us  [run(): pl.pallas_call(kernel, out_shape=(jax.ShapeDtypeStruct((4, ROWS, D // 4),...]
where the time goes in v2:
time: 354 us
  Pallas kernels  331 us (94%)
  local copies, waits for them, and re-layouts  14.1 us (4%)
  matrix products  7 us (2%)
    pallas_call x1, Pallas kernels, run(): pl.pallas_call(kernel, out_shape=(jax.ShapeDtypeStruct((4, ROWS, D // 4),...  331 us
    dynamic_slice x1, local copies, waits for them, and re-layouts, on_device(): mine = lax.dynamic_index_in_dim(frames_in, clip, 0, keepdims=False)  9.12 us

profile of v2, /device:TPU:1, one launch (start us, length us, event | category | flops | bytes accessed | tf_op | source)
XLA Modules:
  0.0 353.6 jit_solution(4282133659046235483)
XLA Ops:
  0.0 9.1 %constant_dynamic-slice_fusion = bf16[1,750,1536]{2,0,1:T(2,128)(2,1)} fusion(bf16[2,750,1536]{2,0,1:T(2,128)(2,1)} %param.6, s32[]{:T(128)S(6)} %select_n.102), kind=kLoop, calls=%fused_computation.62 | loop fusion | bytes 4608004 | tf_op jit(solution)/shard_map/jit(dynamic_index_in_dim)/dynamic_slice | solution.py:325
  9.1 0.0 copy-start.3
  9.1 0.0 copy-start
  9.1 0.0 copy-start.1
  9.1 0.0 copy-start.2
  9.2 5.0 %convolution_convert_fusion.x_ref = bf16[512,1536]{1,0:T(8,128)(2,1)} fusion(bf16[1,750,1536]{2,0,1:T(2,128)(2,1)} %constant_dynamic-slice_fusion, s32[512]{0:T(512)S(1)} %fusion.35), kind=kOutput, calls=%fused_computation.3 | convolution fusion | flops 1180818432 | bytes 3878912 | tf_op jit(solution)/shard_map/dot_general | solution.py:326
  14.1 0.0 copy-done.3
  14.1 0.6 dynamic_slice.9
  14.7 0.7 compare_convert_fusion
  15.4 0.8 broadcast_in_dim.4.mask_ref
  16.2 0.0 copy-done
  16.3 0.1 pad.5.clone
  16.3 0.0 copy-done.1
  16.3 0.0 copy-done.2
  16.3 0.9 maximum_maximum_fusion.prm_ref
  17.2 330.7 %shard_map.64 = (bf16[4,512,384]{2,1,0:T(8,128)(2,1)}, bf16[2,4,2,4,4,48,3072]{6,5,4,3,2,1,0:T(8,128)(2,1)}) custom-call(bf16[512,1536]{1,0:T(8,128)(2,1)} %convolution_convert_fusion.x_ref, f32[512,128]{1,0:T(8,128)} %broadcast_in_dim.4.mask_ref, f32[2,40,1536]{2,1,0:T(8,128)} %maximum_maximum_fusion.prm_ref, bf16[2,48,3072]{2,1,0:T(8,128)(2,1)} %bitcast.19), custom_call_target="tpu_custom_call" | custom-call | tf_op jit(solution)/shard_map/pallas_call | solution.py:302
  347.9 1.5 fusion.40
  349.5 1.0 fusion.6
  350.5 1.0 fusion.7
  351.5 0.1 pad_maximum_fusion
  351.7 1.9 copy.9
  (4 shorter events, 0.1 us)
Async XLA Ops:
  9.1 5.0 %copy-start.3 = (s32[2]{0:T(128)S(1)}, s32[2]{0:T(128)}, u32[]{:S(2)}) copy-start(s32[2]{0:T(128)} %param.7) | copy-start | bytes 28
  9.1 7.1 %copy-start = (f32[2,1,31,1536]{3,1,2,0:T(1,128)S(1)}, f32[2,1,31,1536]{3,1,2,0:T(1,128)}, u32[]{:S(2)}) copy-start(f32[2,1,31,1536]{3,1,2,0:T(1,128)} %param.10) | copy-start | bytes 1142788
  9.1 7.2 %copy-start.1 = (f32[2,1,1536]{2,1,0:T(1,128)S(1)}, f32[2,1,1536]{2,1,0:T(1,128)}, u32[]{:S(2)}) copy-start(f32[2,1,1536]{2,1,0:T(1,128)} %param.11) | copy-start | bytes 36868
  9.1 7.2 %copy-start.2 = (f32[2,1,1536]{2,1,0:T(1,128)S(1)}, f32[2,1,1536]{2,1,0:T(1,128)}, u32[]{:S(2)}) copy-start(f32[2,1,1536]{2,1,0:T(1,128)} %param.8) | copy-start | bytes 36868

commit v3 on v2

--- a/solution.py
+++ b/solution.py
@@ -7,7 +7,7 @@
 from jax.experimental.pallas import tpu as pltpu
 from jax.sharding import PartitionSpec as P
 
-ROWS = 512; LANES = 16; SEG = ROWS // LANES; D = 1536; TAPS = 31; HALF = 15; EPS = 1e-5
+ROWS = 384; LANES = 16; SEG = ROWS // LANES; D = 1536; TAPS = 31; HALF = 15; EPS = 1e-5
 f32 = jnp.float32
 bf16 = jnp.bfloat16
 GROUP, NB = 8, 8
@@ -18,10 +18,31 @@
 class Module:
     def __init__(s, st, mask, prm, wb, norm, gpads, mix):
         s.st, s.mask, s.prm, s.wb, s.norm, s.gpads, s.mix = st, mask, prm, wb, norm, gpads, mix
-    def par(s, m, row, n=1):
-        return s.prm.at[lax.rem(m, jnp.int32(4)), lax.div(m, jnp.int32(4)), row:row + n]
+    def edges(s, g, box, send, recv):
+        s.g, s.box, s.esend, s.erecv = g, box, send, recv
+    def edge(s, m, j, core):
+        over = s.over
+        part = s.gpads[j % 3].at[:, 16 + over:31 + over, 0:8] if core == 1 else s.gpads[j % 3].at[:, 16 + SEG - over - HALF:16 + SEG - over, 8:16]
+        slot = lax.rem(m, jnp.int32(2))
+        return pltpu.make_async_remote_copy(part, s.box.at[slot, j], s.esend.at[slot, j], s.erecv.at[slot, j], device_id=dev(s.g.x, s.g.y, s.g.z, 1 - s.g.core), device_id_type=MESH)
+    def give(s, m, j):
+        for core in range(2):
+            @pl.when(s.g.core == core)
+            def _(): s.edge(m, j, core).start()
+    def take(s, m, j):
+        slot = lax.rem(m, jnp.int32(2)); pad = s.gpads[j % 3]
+        for core in range(2):
+            @pl.when(s.g.core == core)
+            def _():
+                s.edge(m, j, core).wait()
+                if core == 0: pad[:, 16 + SEG:31 + SEG, LANES - 1:LANES] = s.box[slot, j, :, :, 0:1]
+                else: pad[:, 1:16, 0:1] = s.box[slot, j, :, :, 7:8]
+    def taps(s, m):
+        return s.prm[0].at[lax.rem(m, jnp.int32(4)), lax.div(m, jnp.int32(4))]
+    def gain(s, m, row):
+        return s.prm[1][lax.rem(m, jnp.int32(4)), lax.div(m, jnp.int32(4)), row:row + 1, :]
     def ln1(s, m):
-        gain = s.par(m, TAPS)[...]
+        gain = s.gain(m, 0)
         @pl.loop(0, ROWS // 32)
         def _(r):
             for h in range(2):
@@ -31,7 +52,7 @@
                 q = lax.rsqrt(jnp.mean(v * v, axis=-1, keepdims=True) + EPS) * s.mask[rows, :1]
                 s.norm[rows, :] = (v * q * gain).astype(bf16)
     def lift(s, m, j):
-        slot = lax.rem(m, jnp.int32(2)); pad = s.gpads[j % 2]
+        slot = lax.rem(m, jnp.int32(2)); pad = s.gpads[j % 3]
         w = lambda c: s.wb[slot, :, :, :, :, c:c + 256].reshape(D, 256)
         a = jnp.dot(s.norm[...], w(j * 256), preferred_element_type=f32)
         b = jnp.dot(s.norm[...], w(D + j * 256), preferred_element_type=f32)
@@ -43,10 +64,10 @@
             pad[q, 1:16] = jnp.where(sub == 0, 0.0, pltpu.roll(g[SEG - HALF:], 1, 1))
             pad[q, 16 + SEG:31 + SEG] = jnp.where(sub == LANES - 1, 0.0, pltpu.roll(g[:HALF], LANES - 1, 1))
     def conv(s, m, j):
-        pad = s.gpads[j % 2]
+        pad = s.gpads[j % 3]
         for q in range(2):
             c = slice(j * 256 + q * 128, j * 256 + q * 128 + 128)
-            taps = s.par(m, 0, 32)
+            taps = s.taps(m)
             w = [jnp.broadcast_to(taps[k:k + 1, c], (LANES, 128)).astype(bf16) for k in range(TAPS)]
             for base in range(0, SEG, NB):
                 acc = [None] * NB
@@ -64,7 +85,7 @@
                 for o in range(NB):
                     s.mix[base + o, :, c] = acc[o]
     def ln2(s, m):
-        gain = s.par(m, TAPS + 1)[...]
+        gain = s.gain(m, 1)
         @pl.loop(0, ROWS // 32)
         def _(r):
             for h in range(2):
@@ -75,11 +96,15 @@
                 y = v * q * gain
                 s.st[rows, :] = (s.st[rows, :].astype(f32) + s.mask[rows, :1] * (y * sigm(y))).astype(bf16)
     def stage(s, m, j):
-        if j > 0: s.conv(m, j - 1)
-        if j < 6: s.lift(m, j)
+        if j >= 2:
+            s.take(m, j - 2)
+            s.conv(m, j - 2)
+        if j < 6:
+            s.lift(m, j)
+            s.give(m, j)
     def run(s, m):
         s.ln1(m)
-        for j in range(7): s.stage(m, j)
+        for j in range(8): s.stage(m, j)
         s.ln2(m)
 
 
@@ -228,11 +253,32 @@
     @pl.when(jnp.logical_and(m >= 0, m < 8))
     def _(): fn(m)
 
+class Tables:
+    def __init__(s, g, mine, full, send, recv):
+        s.g, s.mine, s.full, s.send, s.recv = g, mine, full, send, recv
+        s.far = dev(g.x, g.y, rem(g.z + 2, 4), g.core)
+        s.near = dev(g.x, g.y, g.z, 1 - g.core)
+        s.across = (1 - g.zh) * 2 + g.core
+    def copy(s, k, n, src, section, to):
+        return pltpu.make_async_remote_copy(src, s.full[n].at[section], s.send.at[k, n], s.recv.at[k, n], device_id=to, device_id_type=MESH)
+    def start(s):
+        for n in range(2):
+            s.copy(0, n, s.mine[n], s.g.sec, s.far).start(); s.copy(1, n, s.mine[n], s.g.sec, s.near).start()
+            s.full[n][s.g.sec] = s.mine[n][...]
+    def relay(s):
+        for n in range(2):
+            s.copy(0, n, s.mine[n], s.across, s.far).wait_recv()
+            s.copy(2, n, s.full[n].at[s.across], s.across, s.near).start()
+    def finish(s):
+        o = 1 - s.g.core
+        for n in range(2):
+            s.copy(1, n, s.mine[n], s.g.zh * 2 + o, s.near).wait_recv()
+            s.copy(2, n, s.mine[n], (1 - s.g.zh) * 2 + o, s.near).wait_recv()
+            for k in range(3): s.copy(k, n, s.mine[n], s.g.sec, s.near).wait_send()
+
 class Shares:
     def __init__(s, g, send, recv, own):
         s.g, s.send, s.recv, s.own = g, send, recv, own
-    def at(s, pipe):
-        return {"pipe": pipe}
     def each(s, src_of, dst_of, what):
         me = s.g.sec
         for q in range(4):
@@ -249,44 +295,49 @@
                 @pl.when(me == q)
                 def _(): pltpu.make_async_copy(src_of(q), dst_of(me), s.own).wait()
 
-def kernel(x_ref, mask_ref, prm_ref, w_ref, out_ref, full, st, wb, norm, gpa, gpb, mix, wsem, prm, ps, pr, po, os_, or_, oo, *sems):
+def kernel(x_ref, mask_ref, taps_ref, gain_ref, w_ref, out_ref, full, st, wb, norm, gpa, gpb, gpc, mix, wsem, taps_all, gain_all, taps_wide, ps, pr, os_, or_, oo, xin, xsem, box, es, er, *sems):
     g = Gather(w_ref, full, sems)
     b = pltpu.get_barrier_semaphore()
     for d in g.peers():
         pl.semaphore_signal(b, inc=1, device_id=d, device_id_type=MESH)
     pl.semaphore_wait(b, len(g.peers()))
-    shares = Shares(g, ps, pr, po)
-    psrc, pdst = (lambda q: prm_ref), (lambda q: prm.at[q])
+    tables = Tables(g, (taps_ref, gain_ref), (taps_all, gain_all), ps, pr)
     g.begin()
     g.e1(jnp.int32(0))
-    shares.each(psrc, pdst, "start")
-    st[...] = x_ref[...]
-    md = Module(st, mask_ref, prm, wb, norm, (gpa, gpb), mix)
+    tables.start()
+    clip = pltpu.make_async_copy(x_ref.at[g.zh], xin, xsem)
+    clip.start()
+    clip.wait()
+    frames = xin.shape[0]
+    p = lax.broadcasted_iota(jnp.int32, (ROWS, frames), 0)
+    when = rem(p, LANES) * SEG + div(p, LANES) + g.core * (frames - ROWS)
+    norm_pick = (when == lax.broadcasted_iota(jnp.int32, (ROWS, frames), 1)).astype(bf16)
+    for j in range(6):
+        c = slice(256 * j, 256 * j + 256)
+        st[:, c] = jnp.dot(norm_pick, xin[:, c], preferred_element_type=f32).astype(bf16)
+    md = Module(st, mask_ref, (taps_wide, gain_all), wb, norm, (gpa, gpb, gpc), mix)
+    md.over = 2 * ROWS - x_ref.shape[1]
+    md.edges(g, box, es, er)
     load = lambda m: pltpu.make_async_copy(full.at[div(m, 4), rem(m, 4)], wb.at[rem(m, 2)], wsem.at[rem(m, 2)])
-    def head(m):
-        g.e6(m); load(m).start()
-        @pl.when(m == 0)
-        def _(): shares.each(psrc, pdst, "wait")
-        md.ln1(m)
+    def ready():
+        tables.finish()
+        taps_wide[...] = taps_all[...].astype(f32)
     def some(m, lo, hi):
         for j in range(lo, hi): md.stage(m, j)
     @pl.loop(0, 14)
     def _(i):
         m = i - 6
-        guard(m, head)
+        @pl.when(i == 2)
+        def _(): tables.relay()
+        @pl.when(i == 5)
+        def _(): ready()
+        guard(m, lambda m: (g.e6(m), load(m).start()))
         @pl.when(i > 0)
         def _(): guard(i, g.e1)
-        guard(i - 1, g.e2)
-        guard(m, lambda m: load(m).wait())
-        guard(m, lambda m: some(m, 0, 2))
-        guard(i - 2, g.e3)
-        guard(m, lambda m: some(m, 2, 4))
-        guard(i - 3, g.e4)
-        guard(m, lambda m: some(m, 4, 5))
-        guard(i - 4, g.e5a)
-        guard(m, lambda m: some(m, 5, 7))
-        guard(m, md.ln2)
-        guard(i - 5, g.e5b)
+        guard(i - 1, g.e2); guard(i - 2, g.e3); guard(i - 3, g.e4); guard(i - 4, g.e5a); guard(i - 5, g.e5b)
+        @pl.when(m >= 0)
+        def _():
+            md.ln1(m); load(m).wait(); some(m, 0, 8); md.ln2(m)
     outs = Shares(g, os_, or_, oo)
     osrc, odst = (lambda q: st.at[:, pl.ds(q * (D // 4), D // 4)]), (lambda q: out_ref.at[q])
     outs.each(osrc, odst, "start")
@@ -297,21 +348,21 @@
 SEM = pltpu.SemaphoreType.DMA
 V = pltpu.VMEM
 
-def run(x, mask, prm, w):
+def run(x, mask, taps, gains, w):
     vm, hbm = pl.BlockSpec(memory_space=pltpu.VMEM), pl.BlockSpec(memory_space=pl.ANY)
     return pl.pallas_call(
         kernel,
         out_shape=(jax.ShapeDtypeStruct((4, ROWS, D // 4), jnp.bfloat16), jax.ShapeDtypeStruct((2, 4, 2, 4, 4, 48, 2 * D), jnp.bfloat16)),
-        in_specs=[vm, vm, vm, vm],
+        in_specs=[hbm, vm, vm, vm, vm],
         out_specs=(hbm, hbm),
         scratch_shapes=[
             V((ROWS, D), jnp.bfloat16), V((2, 2, 4, 4, 48, 2 * D), jnp.bfloat16), V((ROWS, D), jnp.bfloat16),
-            V((2, 32 + SEG, LANES, 128), f32), V((2, 32 + SEG, LANES, 128), f32), V((SEG, LANES, D), f32), SEM((2,)), V((4, 2, 40, D), f32),
-            SEM((4,)), SEM((4,)), SEM, SEM((4,)), SEM((4,)), SEM,
+            V((2, 32 + SEG, LANES, 128), f32), V((2, 32 + SEG, LANES, 128), f32), V((2, 32 + SEG, LANES, 128), f32), V((SEG, LANES, D), f32), SEM((2,)), V((4, 2, 32, D), bf16), V((4, 2, 8, D), f32), V((4, 2, 32, D), f32),
+            SEM((3, 2)), SEM((3, 2)), SEM((4,)), SEM((4,)), SEM, V(x.shape[1:], bf16), SEM, V((2, 6, 2, HALF, 8, 128), f32), SEM((2, 6)), SEM((2, 6)),
             SEM((3,)), SEM((8, 3)), SEM((8, 2)), SEM((8, 3)), SEM((8, 3)), SEM((8, 3, 4)), SEM((8, 3, 4)), SEM((8, 3, 4)), SEM((8, 3, 4)), SEM((8, 3)), SEM((8, 3)),
         ],
         compiler_params=pltpu.CompilerParams(collective_id=0, has_side_effects=True, vmem_limit_bytes=60 * 2**20),
-    )(x, mask, prm, w)[0]
+    )(x, mask, taps, gains, w)[0]
 
 def on_device(frames_in, lengths, norm_gain, lift_weight, depth_kernel, out_gain):
     frames = frames_in.shape[1]
@@ -321,13 +372,11 @@
     p = jnp.arange(ROWS, dtype=jnp.int32)
     local = p % LANES * SEG + p // LANES
     when = local + half * late
-    pick = (when[:, None] == jnp.arange(frames, dtype=jnp.int32)[None]).astype(jnp.bfloat16)
-    mine = lax.dynamic_index_in_dim(frames_in, clip, 0, keepdims=False)
-    x = jnp.dot(pick, mine, preferred_element_type=f32).astype(jnp.bfloat16)
     length = lax.dynamic_index_in_dim(lengths, clip, 0, keepdims=False)
     mask = jnp.broadcast_to((when < length).astype(f32)[:, None], (ROWS, 128))
-    prm = jnp.concatenate([depth_kernel[:, 0], norm_gain, out_gain, jnp.zeros((2, 7, D), f32)], axis=1)
-    got = run(x, mask, prm, lift_weight[:, 0])
+    taps = jnp.pad(depth_kernel[:, 0].astype(bf16), ((0, 0), (0, 1), (0, 0)))
+    gains = jnp.concatenate([norm_gain, out_gain, jnp.zeros((2, 6, D), f32)], axis=1)
+    got = run(frames_in, mask, taps, gains, lift_weight[:, 0])
     t = jnp.arange(frames, dtype=jnp.int32)
     cut = frames // 2
     source = jnp.where(t < cut, local_row(t), ROWS + local_row(t - late))

time: 354 us -> 278 us (0.79)
  Pallas kernels: 331 us -> 263 us
  matrix products: 7 us -> 1.62 us
    pallas_call x1, Pallas kernels: 331 us -> 263 us  [run(): pl.pallas_call(kernel, out_shape=(jax.ShapeDtypeStruct((4, ROWS, D // 4),...]
    dynamic_slice x1 -> x0, local copies, waits for them, and re-layouts: 9.12 us -> none  [on_device(): mine = lax.dynamic_index_in_dim(frames_in, clip, 0, keepdims=False)]
    unnamed x9 -> x8, local copies, waits for them, and re-layouts: 0.05 us -> 5.22 us
    dot_general x1 -> x0, matrix products: 4.98 us -> none  [on_device(): x = jnp.dot(pick, mine, preferred_element_type=f32).astype(jnp.bfloat16)]
where the time goes in v3:
time: 278 us
  Pallas kernels  263 us (95%)
  local copies, waits for them, and re-layouts  11.3 us (4%)
    pallas_call x1, Pallas kernels, run(): pl.pallas_call(kernel, out_shape=(jax.ShapeDtypeStruct((4, ROWS, D // 4),...  263 us

profile of v3, /device:TPU:1, one launch (start us, length us, event | category | flops | bytes accessed | tf_op | source)
XLA Modules:
  0.0 277.7 jit_solution(3404853059093237585)
XLA Ops:
  0.0 1.2 dynamic_slice.4
  1.2 0.7 fusion.41
  1.9 0.8 broadcast_in_dim.4.mask_ref
  2.7 0.0 copy-start
  2.7 0.0 copy-start.1
  2.7 0.0 copy-start.2
  2.7 5.2 %copy.8.x_ref = bf16[2,750,1536]{2,1,0:T(8,128)(2,1)} copy(bf16[2,750,1536]{2,0,1:T(2,128)(2,1)} %param.6) | data formatting | bytes 9216000 | tf_op args[0]
  7.9 0.0 copy-done
  7.9 0.7 pad.4.taps_ref
  8.6 0.1 pad.9.clone
  8.7 0.0 copy-done.1
  8.7 0.0 copy-done.2
  8.7 0.7 maximum_maximum_fusion.gain_ref
  9.4 263.2 %shard_map.64 = (bf16[4,384,384]{2,1,0:T(8,128)(2,1)}, bf16[2,4,2,4,4,48,3072]{6,5,4,3,2,1,0:T(8,128)(2,1)}) custom-call(bf16[2,750,1536]{2,1,0:T(8,128)(2,1)} %copy.8.x_ref, f32[384,128]{1,0:T(8,128)} %broadcast_in_dim.4.mask_ref, bf16[2,32,1536]{2,1,0:T(8,128)(2,1)} %pad.4.taps_ref, f32[2,8,1536]{2,1,0:T(8,128)} %maximum_maximum_fusion.gain_ref, ...), custom_call_target="tpu_custom_call" | custom-call | tf_op jit(solution)/shard_map/pallas_call | solution.py:353
  272.6 1.4 fusion.44
  274.0 0.8 fusion.4
  274.8 0.8 fusion.5
  275.6 0.1 pad_maximum_fusion
  275.8 1.9 copy.9
  (3 shorter events, 0.0 us)
Async XLA Ops:
  2.7 5.2 %copy-start = (f32[2,1,31,1536]{3,1,2,0:T(1,128)S(1)}, f32[2,1,31,1536]{3,1,2,0:T(1,128)}, u32[]{:S(2)}) copy-start(f32[2,1,31,1536]{3,1,2,0:T(1,128)} %param.10) | copy-start | bytes 1142788
  2.7 6.0 %copy-start.1 = (f32[2,1,1536]{2,1,0:T(1,128)S(1)}, f32[2,1,1536]{2,1,0:T(1,128)}, u32[]{:S(2)}) copy-start(f32[2,1,1536]{2,1,0:T(1,128)} %param.11) | copy-start | bytes 36868
  2.7 6.0 %copy-start.2 = (f32[2,1,1536]{2,1,0:T(1,128)S(1)}, f32[2,1,1536]{2,1,0:T(1,128)}, u32[]{:S(2)}) copy-start(f32[2,1,1536]{2,1,0:T(1,128)} %param.8) | copy-start | bytes 36868

commit v4 on v3

--- a/solution.py
+++ b/solution.py
@@ -108,7 +108,7 @@
         s.ln2(m)
 
 
-SPLIT = (4, 5, 3)
+SPLIT = ((2, 3, 1), (2, 2, 2))
 MESH = pl.DeviceIdType.MESH
 
 def div(a, b): return lax.div(a, jnp.int32(b))
@@ -153,7 +153,10 @@
         (s.own_sem, s.zs, s.zr, s.cs, s.cr, s.ms, s.mr, s.fs, s.fr, s.ds, s.dr) = sems
     def cols(s, part, n=1, core=None):
         core = s.core if core is None else core
-        return pl.ds(pl.multiple_of(core * 1536 + 128 * sum(SPLIT[:part]), 128), 128 * sum(SPLIT[part:part + n]))
+        split = SPLIT[s.half]
+        return pl.ds(pl.multiple_of(core * D + s.half * (D // 2) + 128 * sum(split[:part]), 128), 128 * sum(split[part:part + n]))
+    def side(s, core):
+        return pl.ds(pl.multiple_of(core * D, 128), D)
     def peers(s):
         x, y, z, c = s.x, s.y, s.z, s.core
         r = [dev(x, y, z, 1 - c)]
@@ -164,21 +167,21 @@
         return r
     def own_copies(s):
         o = 1 - s.core
-        mine, other = s.cols(0, 3), s.cols(0, 3, o)
+        mine, other = s.side(s.core), s.side(o)
         here = s.full.at[:, s.sec, s.zl, s.x, s.y]
         return (pltpu.make_async_copy(s.w.at[:, :, mine], here.at[:, :, mine], s.own_sem.at[0]),
                 pltpu.make_async_remote_copy(s.w.at[:, :, other], here.at[:, :, other], s.own_sem.at[1], s.own_sem.at[2], device_id=dev(s.x, s.y, s.z, o), device_id_type=MESH))
     def own_arrival(s):
-        mine = s.cols(0, 3)
+        mine = s.side(s.core)
         there = s.full.at[:, s.zh * 2 + 1 - s.core, s.zl, s.x, s.y]
         return pltpu.make_async_remote_copy(s.w.at[:, :, mine], there.at[:, :, mine], s.own_sem.at[1], s.own_sem.at[2], device_id=dev(s.x, s.y, s.z, 1 - s.core), device_id_type=MESH)
     def begin(s):
         a, b = s.own_copies()
         a.start(); b.start(); a.wait(); b.wait_send(); s.own_arrival().wait_recv()
     def mod(s, c):
-        return s.full.at[div(c, 4), rem(c, 4)]
+        return s.full.at[div(c, 8), rem(div(c, 2), 4)]
     def src(s, c):
-        return s.zh == div(rem(c, 4), 2)
+        return s.zh == div(rem(div(c, 2), 4), 2)
     def first_sends(s, c):
         W = s.mod(c); out = []
         for d in (1, 2, 3):
@@ -216,7 +219,7 @@
         return [Ring(s.y, aty, lambda q: W.at[:, :, q, :, a], lambda q, h: W.at[h, :, q, :, a], yes, s.fs.at[c, 0], s.fr.at[c, 0]),
                 Ring(s.x, atx, lambda q: W.at[:, q, :, :, b], lambda q, h: W.at[h, q, :, :, b], yes, s.fs.at[c, 1], s.fr.at[c, 1]),
                 Ring(s.z, atz, lambda q: W.at[rem(q, 2), :, :, :, cc], lambda q, h: W.at[rem(q, 2), pl.ds(2 * h, 2), :, :, cc],
-                     lambda q: div(q, 2) == div(rem(c, 4), 2), s.fs.at[c, 2], s.fr.at[c, 2])]
+                     lambda q: div(q, 2) == div(rem(div(c, 2), 4), 2), s.fs.at[c, 2], s.fr.at[c, 2])]
     def swap(s, c, part, core):
         sl = s.mod(c).at[:, :, :, :, s.cols(part, 1, core)]
         return pltpu.make_async_remote_copy(sl, sl, s.ds.at[c, part], s.dr.at[c, part], device_id=dev(s.x, s.y, s.z, 1 - s.core), device_id_type=MESH)
@@ -250,7 +253,7 @@
 
 
 def guard(m, fn):
-    @pl.when(jnp.logical_and(m >= 0, m < 8))
+    @pl.when(jnp.logical_and(m >= 0, m < 16))
     def _(): fn(m)
 
 class Tables:
@@ -303,6 +306,7 @@
     pl.semaphore_wait(b, len(g.peers()))
     tables = Tables(g, (taps_ref, gain_ref), (taps_all, gain_all), ps, pr)
     g.begin()
+    g.half = 0
     g.e1(jnp.int32(0))
     tables.start()
     clip = pltpu.make_async_copy(x_ref.at[g.zh], xin, xsem)
@@ -318,31 +322,53 @@
     md = Module(st, mask_ref, (taps_wide, gain_all), wb, norm, (gpa, gpb, gpc), mix)
     md.over = 2 * ROWS - x_ref.shape[1]
     md.edges(g, box, es, er)
-    load = lambda m: pltpu.make_async_copy(full.at[div(m, 4), rem(m, 4)], wb.at[rem(m, 2)], wsem.at[rem(m, 2)])
+    def load(m, half, what):
+        slot = rem(m, 2)
+        for k in range(2):
+            c = pl.ds(k * D + half * (D // 2), D // 2)
+            getattr(pltpu.make_async_copy(full.at[div(m, 4), rem(m, 4), :, :, :, :, c], wb.at[slot, :, :, :, :, c], wsem.at[slot, half, k]), what)()
     def ready():
         tables.finish()
         taps_wide[...] = taps_all[...].astype(f32)
     def some(m, lo, hi):
         for j in range(lo, hi): md.stage(m, j)
-    @pl.loop(0, 14)
+    @pl.loop(0, 12)
     def _(i):
-        m = i - 6
-        @pl.when(i == 2)
-        def _(): tables.relay()
-        @pl.when(i == 5)
-        def _(): ready()
-        guard(m, lambda m: (g.e6(m), load(m).start()))
-        @pl.when(i > 0)
-        def _(): guard(i, g.e1)
-        guard(i - 1, g.e2); guard(i - 2, g.e3); guard(i - 3, g.e4); guard(i - 4, g.e5a); guard(i - 5, g.e5b)
-        @pl.when(m >= 0)
-        def _():
-            md.ln1(m); load(m).wait(); some(m, 0, 8); md.ln2(m)
+        for half in range(2):
+            n = 2 * i + half
+            part, m = 1 - half, i - 4 + half
+            def event(after, fn):
+                g.half = (half - after) % 2
+                guard(n - after, fn)
+            @pl.when(n == 4)
+            def _(): tables.relay()
+            @pl.when(n == 5)
+            def _(): ready()
+            def fetch(k):
+                g.e6(k)
+                load(m, part, "start")
+            event(7, fetch)
+            @pl.when(n > 0)
+            def _(): event(0, g.e1)
+            event(1, g.e2)
+            event(2, g.e3)
+            event(3, g.e4)
+            event(4, g.e5a)
+            def compute(k):
+                if part == 0: md.ln1(m)
+                load(m, part, "wait")
+                some(m, 3 * part, 3 + 5 * part)
+                if part == 1: md.ln2(m)
+            event(7, compute)
+            event(5, g.e5b)
     outs = Shares(g, os_, or_, oo)
     osrc, odst = (lambda q: st.at[:, pl.ds(q * (D // 4), D // 4)]), (lambda q: out_ref.at[q])
     outs.each(osrc, odst, "start")
     @pl.loop(0, 8)
-    def _(i): g.drain(i)
+    def _(i):
+        for half in range(2):
+            g.half = half
+            g.drain(2 * i + half)
     outs.each(osrc, odst, "wait")
 
 SEM = pltpu.SemaphoreType.DMA
@@ -357,9 +383,9 @@
         out_specs=(hbm, hbm),
         scratch_shapes=[
             V((ROWS, D), jnp.bfloat16), V((2, 2, 4, 4, 48, 2 * D), jnp.bfloat16), V((ROWS, D), jnp.bfloat16),
-            V((2, 32 + SEG, LANES, 128), f32), V((2, 32 + SEG, LANES, 128), f32), V((2, 32 + SEG, LANES, 128), f32), V((SEG, LANES, D), f32), SEM((2,)), V((4, 2, 32, D), bf16), V((4, 2, 8, D), f32), V((4, 2, 32, D), f32),
+            V((2, 32 + SEG, LANES, 128), f32), V((2, 32 + SEG, LANES, 128), f32), V((2, 32 + SEG, LANES, 128), f32), V((SEG, LANES, D), f32), SEM((2, 2, 2)), V((4, 2, 32, D), bf16), V((4, 2, 8, D), f32), V((4, 2, 32, D), f32),
             SEM((3, 2)), SEM((3, 2)), SEM((4,)), SEM((4,)), SEM, V(x.shape[1:], bf16), SEM, V((2, 6, 2, HALF, 8, 128), f32), SEM((2, 6)), SEM((2, 6)),
-            SEM((3,)), SEM((8, 3)), SEM((8, 2)), SEM((8, 3)), SEM((8, 3)), SEM((8, 3, 4)), SEM((8, 3, 4)), SEM((8, 3, 4)), SEM((8, 3, 4)), SEM((8, 3)), SEM((8, 3)),
+            SEM((3,)), SEM((16, 3)), SEM((16, 2)), SEM((16, 3)), SEM((16, 3)), SEM((16, 3, 4)), SEM((16, 3, 4)), SEM((16, 3, 4)), SEM((16, 3, 4)), SEM((16, 3)), SEM((16, 3)),
         ],
         compiler_params=pltpu.CompilerParams(collective_id=0, has_side_effects=True, vmem_limit_bytes=60 * 2**20),
     )(x, mask, taps, gains, w)[0]

time: 278 us -> 268 us (0.964)
  Pallas kernels: 263 us -> 253 us
    pallas_call x1, Pallas kernels: 263 us -> 253 us  [run(): pl.pallas_call(kernel, out_shape=(jax.ShapeDtypeStruct((4, ROWS, D // 4),...]
where the time goes in v4:
time: 268 us
  Pallas kernels  253 us (94%)
  local copies, waits for them, and re-layouts  11.3 us (4%)
    pallas_call x1, Pallas kernels, run(): pl.pallas_call(kernel, out_shape=(jax.ShapeDtypeStruct((4, ROWS, D // 4),...  253 us

profile of v4, /device:TPU:1, one launch (start us, length us, event | category | flops | bytes accessed | tf_op | source)
XLA Modules:
  0.0 267.7 jit_solution(3306417764538502783)
XLA Ops:
  0.0 1.2 dynamic_slice.4
  1.2 0.7 fusion.41
  1.9 0.8 broadcast_in_dim.4.mask_ref
  2.7 0.0 copy-start
  2.7 0.0 copy-start.1
  2.7 0.0 copy-start.2
  2.7 5.2 %copy.8.x_ref = bf16[2,750,1536]{2,1,0:T(8,128)(2,1)} copy(bf16[2,750,1536]{2,0,1:T(2,128)(2,1)} %param.6) | data formatting | bytes 9216000 | tf_op args[0]
  7.9 0.0 copy-done
  7.9 0.7 pad.4.taps_ref
  8.6 0.1 pad.9.clone
  8.7 0.0 copy-done.1
  8.7 0.0 copy-done.2
  8.7 0.7 maximum_maximum_fusion.gain_ref
  9.4 253.2 %shard_map.64 = (bf16[4,384,384]{2,1,0:T(8,128)(2,1)}, bf16[2,4,2,4,4,48,3072]{6,5,4,3,2,1,0:T(8,128)(2,1)}) custom-call(bf16[2,750,1536]{2,1,0:T(8,128)(2,1)} %copy.8.x_ref, f32[384,128]{1,0:T(8,128)} %broadcast_in_dim.4.mask_ref, bf16[2,32,1536]{2,1,0:T(8,128)(2,1)} %pad.4.taps_ref, f32[2,8,1536]{2,1,0:T(8,128)} %maximum_maximum_fusion.gain_ref, ...), custom_call_target="tpu_custom_call" | custom-call | tf_op jit(solution)/shard_map/pallas_call | solution.py:379
  262.7 1.4 fusion.44
  264.0 0.8 fusion.4
  264.9 0.8 fusion.5
  265.7 0.1 pad_maximum_fusion
  265.8 1.9 copy.9
  (3 shorter events, 0.0 us)
Async XLA Ops:
  2.7 5.2 %copy-start = (f32[2,1,31,1536]{3,1,2,0:T(1,128)S(1)}, f32[2,1,31,1536]{3,1,2,0:T(1,128)}, u32[]{:S(2)}) copy-start(f32[2,1,31,1536]{3,1,2,0:T(1,128)} %param.10) | copy-start | bytes 1142788
  2.7 6.0 %copy-start.1 = (f32[2,1,1536]{2,1,0:T(1,128)S(1)}, f32[2,1,1536]{2,1,0:T(1,128)}, u32[]{:S(2)}) copy-start(f32[2,1,1536]{2,1,0:T(1,128)} %param.11) | copy-start | bytes 36868
  2.7 6.0 %copy-start.2 = (f32[2,1,1536]{2,1,0:T(1,128)S(1)}, f32[2,1,1536]{2,1,0:T(1,128)}, u32[]{:S(2)}) copy-start(f32[2,1,1536]{2,1,0:T(1,128)} %param.8) | copy-start | bytes 36868
